TPU v7x, 32 devices: a whole 2x2x4 slice. The times are simulated.
32 devices in a mesh: pts: 4 (over y, core), grid: 8 (over z, x).
Axes of the slice: x: 2, y: 2, z: 4, core: 2. Of those that a mesh axis runs over, the one named last changes fastest.
Arguments:
- features: bfloat16 [32, 524288], P(None, ('pts', 'grid')), may hold values from -6 to 6
- w_in: bfloat16 [32, 64], replicated, may hold values from -1 to 1
- w_mid: bfloat16 [64, 64], replicated, may hold values from -0.75 to 0.75
- w_conv: bfloat16 [2, 3, 3, 3, 64, 64], replicated, may hold values from -0.15625 to 0.15625
- point_frac: float32 [3, 524288], P(None, ('pts', 'grid')), may hold values from 0 to 1
- point_base: int32 [3, 524288], P(None, ('pts', 'grid')), may hold values from 0 to 6, as said below
- slot_dest: int32 [2048], P(('pts', 'grid')), may hold values from 0 to 7, as said below
- slot_tile_block: int32 [2048], P(('pts', 'grid')), may hold values from 0 to 63
- slot_count: int32 [2048], P(('pts', 'grid')), may hold values from 1 to 256, as said below
Outputs:
- point_out: bfloat16 [64, 524288], P(None, ('pts', 'grid'))
Inputs may be any that keep to these rules, and one draw needn't show every extreme that they name: `point_base`: the three rows give base cells along the first, second and third dimension; the first two rows lie in 0 .. 2 and the third in 0 .. 6, so all eight corners of a point lie in its block. `slot_dest`: among the 64 slots of one device at most 16 name the same value; on every device one value is named by exactly 16 slots, the same value on all devices of one index along pts. `slot_count`: every device has a slot with exactly 256 live points.
All inputs are finite; a program needn't handle non-finite values.
Results may differ from a plain program's by a relative error of at most 0.0035.
The roundings to bfloat16 on the way count: a program that leaves them out, or rounds other values in their place, can miss the bound.
Values may be sent and summed in bfloat16 or wider, within the bound.
A program may use at most 128 MiB of HBM per device.

v0:
```python
import functools

import jax
import jax.numpy as jnp
import numpy as np
from jax import lax
from jax.experimental import pallas as pl
from jax.experimental.pallas import tpu as pltpu
from jax.sharding import PartitionSpec as P

GZ = 8
BLOCK_EDGE_CELLS = 4
TX = 32
TY = 32
ID_LANES = 128
MESH = pl.DeviceIdType.MESH
DIRECTIONS = ((1, 0), (-1, 0), (0, 1), (0, -1), (1, 1), (1, -1), (-1, 1), (-1, -1))


def point_layer(weight, inputs):
    mixed_sum = lax.dot_general(
        weight, inputs, (((0,), (0,)), ((), ())), preferred_element_type=jnp.float32
    )
    return jax.nn.silu(mixed_sum).astype(jnp.bfloat16)


def axis_weights(offset, corner, positions):
    positions = positions[:, None, None]
    below_part = jnp.where(positions == corner[None], 1.0 - offset[None], 0.0)
    above_part = jnp.where(positions == corner[None] + 1, offset[None], 0.0)
    return below_part + above_part


def trilinear(offsets, corners, counts, block_edge, grid_depth):
    slot_width = offsets.shape[2]
    live_mask = (jnp.arange(slot_width, dtype=jnp.int32)[None, :] < counts[:, None]).astype(
        jnp.float32
    )
    cells = jnp.arange(block_edge * block_edge, dtype=jnp.int32)
    along_x = axis_weights(offsets[0], corners[0], cells // block_edge)
    along_y = axis_weights(offsets[1], corners[1], cells % block_edge)
    along_z = axis_weights(offsets[2], corners[2], jnp.arange(grid_depth, dtype=jnp.int32))
    corner_weights = (along_x * along_y)[:, None] * along_z[None] * live_mask
    return corner_weights.astype(jnp.bfloat16)


def splat(weights, hidden):
    sums = jnp.einsum("czsp,hsp->sczh", weights, hidden, preferred_element_type=jnp.float32)
    return sums.astype(jnp.bfloat16).reshape(sums.shape[0], sums.shape[1], -1)


def interpolate(weights, blocks):
    cells = blocks.reshape(blocks.shape[0], weights.shape[0], weights.shape[1], -1)
    return jnp.einsum("czsp,sczh->hsp", weights, cells, preferred_element_type=jnp.float32).astype(
        jnp.bfloat16
    )


def build_band(w_ref, band_ref):
    width = w_ref.shape[2]
    depth = band_ref.shape[1] // width

    def one(n, carry):
        band_ref[n] = jnp.zeros(band_ref.shape[1:], band_ref.dtype)
        for b in range(depth):
            low, high = max(b - 1, 0), min(b + 2, depth)
            band_ref[n, low * width : high * width, b * width : (b + 1) * width] = w_ref[
                n, (low - b + 1) * width : (high - b + 1) * width, :
            ]
        return carry

    lax.fori_loop(0, band_ref.shape[0], one, 0)


def halo_selectors():
    edge, nbx, nby = BLOCK_EDGE_CELLS, TX // BLOCK_EDGE_CELLS, TY // BLOCK_EDGE_CELLS
    blocks = nbx * nby
    lane = edge * max(nbx, nby)
    cut_sides = np.zeros((4, lane, edge * blocks), np.float32)
    cut_corners = np.zeros((4, lane, blocks), np.float32)
    for k, (da, db) in enumerate(DIRECTIONS):
        bx, by = (nbx - 1 if da > 0 else 0), (nby - 1 if db > 0 else 0)
        if db == 0:
            for j in range(edge):
                for y in range(nby):
                    cut_sides[k, j * nby + y, j * blocks + bx * nby + y] = 1
        elif da == 0:
            for i in range(edge):
                for x in range(nbx):
                    cut_sides[k, i * nbx + x, i * blocks + x * nby + by] = 1
        else:
            cut_corners[k - 4, :, bx * nby + by] = 1
    put_sides = np.zeros((4, edge, blocks, blocks + lane), np.float32)
    put_corners = np.zeros((4, blocks, blocks + 3 * lane), np.float32)
    for k, (da, db) in enumerate(DIRECTIONS):
        for x in range(nbx):
            for y in range(nby):
                row, sx, sy = x * nby + y, x - da, y - db
                out_x, out_y = not 0 <= sx < nbx, not 0 <= sy < nby
                if da == 0 or db == 0:
                    for phase in range(edge):
                        if out_x:
                            column = blocks + phase * nby + sy
                        elif out_y:
                            column = blocks + phase * nbx + sx
                        else:
                            column = sx * nby + sy
                        put_sides[k, phase, row, column] = 1
                else:
                    i, j = (edge - 1 if da > 0 else 0), (edge - 1 if db > 0 else 0)
                    if out_x and out_y:
                        column = blocks + 2 * lane
                    elif out_x:
                        column = blocks + j * nby + sy
                    elif out_y:
                        column = blocks + lane + i * nbx + sx
                    else:
                        column = sx * nby + sy
                    put_corners[k - 4, row, column] = 1
    return [jnp.asarray(m, jnp.bfloat16) for m in (cut_sides, cut_corners, put_sides, put_corners)]


def select(one_hot, values):
    return jnp.dot(one_hot, values, preferred_element_type=jnp.float32).astype(jnp.bfloat16)


def conv_kernel(
    sizes,
    ids_ref,
    send_picks,
    sums_ref,
    w_ref,
    cut_sides,
    cut_corners,
    put_sides,
    put_corners,
    out_ref,
    ids,
    outgoing,
    arrived,
    values,
    returned,
    totals,
    band_ref,
    phases,
    around,
    leaving,
    landing,
    send_sem,
    recv_sem,
    id_send,
    id_recv,
    go_send,
    go_recv,
    back_send,
    back_recv,
    own_sem,
):
    rows, columns = sizes
    edge, blocks, every = BLOCK_EDGE_CELLS, phases.shape[2], phases.shape[3]
    layers = landing.shape[0]
    me_row, me_column = lax.axis_index("grid"), lax.axis_index("pts")

    def present(da, db):
        row, column = me_row + da, me_column + db
        return (row >= 0) & (row < rows) & (column >= 0) & (column < columns)

    def tell(t):
        owner = lax.rem(me_row + t, rows)
        return pltpu.make_async_remote_copy(
            src_ref=ids_ref.at[owner],
            dst_ref=ids.at[me_row],
            send_sem=id_send.at[t],
            recv_sem=id_recv.at[t],
            device_id=(me_column, owner),
            device_id_type=MESH,
        )

    def go(i, t):
        owner = lax.rem(me_row + t, rows)
        part = pl.ds(i * edge * every, edge * every)
        return pltpu.make_async_remote_copy(
            src_ref=outgoing.at[owner, :, part],
            dst_ref=arrived.at[me_row, :, part],
            send_sem=go_send.at[i, t],
            recv_sem=go_recv.at[i, t],
            device_id=(me_column, owner),
            device_id_type=MESH,
        )

    def back(i, t):
        origin = lax.rem(me_row + t, rows)
        part = pl.ds(i * edge * every, edge * every)
        return pltpu.make_async_remote_copy(
            src_ref=values.at[origin, :, part],
            dst_ref=returned.at[me_row, :, part],
            send_sem=back_send.at[i, t],
            recv_sem=back_recv.at[i, t],
            device_id=(me_column, origin),
            device_id_type=MESH,
        )

    def back_own(i):
        part = pl.ds(i * edge * every, edge * every)
        return pltpu.make_async_copy(
            values.at[me_row, :, part], returned.at[me_row, :, part], own_sem.at[i + 1]
        )

    barrier = pltpu.get_barrier_semaphore()
    for t in range(1, rows):
        pl.semaphore_signal(
            barrier,
            inc=1,
            device_id=(me_column, lax.rem(me_row + t, rows)),
            device_id_type=MESH,
        )
    for da, db in DIRECTIONS:
        if db != 0:

            @pl.when(present(da, db))
            def _():
                pl.semaphore_signal(
                    barrier, inc=1, device_id=(me_column + db, me_row + da), device_id_type=MESH
                )

    tall = 3 - (me_row == 0).astype(jnp.int32) - (me_row == rows - 1).astype(jnp.int32)
    wide = 2 - (me_column == 0).astype(jnp.int32) - (me_column == columns - 1).astype(jnp.int32)
    pl.semaphore_wait(barrier, rows - 1 + tall * wide)

    for t in range(1, rows):
        tell(t).start()
    for i in range(edge):
        for j in range(edge):
            lanes = slice((i * edge + j) * every, (i * edge + j + 1) * every)
            outgoing[:, :, lanes] = select(send_picks[...], sums_ref[:, lanes]).reshape(
                outgoing.shape[0], outgoing.shape[1], every
            )
        for t in range(1, rows):
            go(i, t).start()
    own = pltpu.make_async_copy(outgoing.at[me_row], arrived.at[me_row], own_sem.at[0])
    own.start()
    ids[me_row] = ids_ref[me_row]
    build_band(w_ref, band_ref)

    def inner_terms(layer, source):
        window = around[source + 1, 1 : edge + 1].reshape(edge * blocks, every)
        for shift_x in range(3):
            i = source + 1 - shift_x
            if 0 <= i < edge:
                term = jnp.dot(
                    window,
                    band_ref[layer * 9 + shift_x * 3 + 1],
                    preferred_element_type=jnp.float32,
                )
                if source == max(i - 1, 0):
                    totals[i] = term
                else:
                    totals[i] += term

    own.wait()
    for t in range(1, rows):
        tell(t).wait_recv()
    queue = arrived.shape[0] * arrived.shape[1]
    named = ids[...].reshape(queue, ID_LANES).astype(jnp.float32)[:, :blocks]
    places = lax.broadcasted_iota(jnp.int32, (queue, blocks), 1).astype(jnp.float32)
    picks = jnp.where(named == places, 1.0, 0.0).astype(jnp.bfloat16)
    for i in range(edge):
        for t in range(1, rows):
            go(i, t).wait_recv()
        for j in range(edge):
            cell = i * edge + j
            phases[i, j] = lax.dot_general(
                picks,
                arrived[:, :, cell * every : (cell + 1) * every].reshape(queue, every),
                (((0,), (0,)), ((), ())),
                preferred_element_type=jnp.float32,
            ).astype(jnp.bfloat16)
        around[i + 1, 1 : edge + 1] = phases[i]
        if i < edge - 1:
            inner_terms(0, i)

    for layer in range(layers):

        def copy(k):
            da, db = DIRECTIONS[k]
            return pltpu.make_async_remote_copy(
                src_ref=leaving.at[layer, k],
                dst_ref=landing.at[layer, k],
                send_sem=send_sem.at[layer, k],
                recv_sem=recv_sem.at[layer, k],
                device_id=(me_column + db, me_row + da),
                device_id_type=MESH,
            )

        for k, (da, db) in enumerate(DIRECTIONS):
            i, j = (edge - 1 if da > 0 else 0), (edge - 1 if db > 0 else 0)
            if db == 0:
                source = phases[i].reshape(edge * blocks, every)
            elif da == 0:
                source = phases[:, j].reshape(edge * blocks, every)
            else:
                source = phases[i, j]
            leaving[layer, k] = select(cut_sides[k] if k < 4 else cut_corners[k - 4], source)

            @pl.when(present(da, db))
            def _():
                copy(k).start()

        if layer == 0:
            inner_terms(0, edge - 1)
        else:
            for i in range(edge):
                around[i + 1, 1 : edge + 1] = phases[i]
                inner_terms(layer, i)
        for k, (da, db) in enumerate(DIRECTIONS):

            @pl.when(present(-da, -db))
            def _():
                copy(k).wait_recv()

            @pl.when(jnp.logical_not(present(-da, -db)))
            def _():
                landing[layer, k] = jnp.zeros(landing.shape[2:], landing.dtype)

        for k, (da, db) in enumerate(DIRECTIONS):
            to_x = 0 if da > 0 else edge + 1
            to_y = 0 if db > 0 else edge + 1
            i, j = (edge - 1 if da > 0 else 0), (edge - 1 if db > 0 else 0)
            if db == 0:
                for phase in range(edge):
                    around[to_x, phase + 1] = select(
                        put_sides[k, phase],
                        jnp.concatenate([phases[i, phase], landing[layer, k]], axis=0),
                    )
            elif da == 0:
                for phase in range(edge):
                    around[phase + 1, to_y] = select(
                        put_sides[k, phase],
                        jnp.concatenate([phases[phase, j], landing[layer, k]], axis=0),
                    )
            else:
                side_x = DIRECTIONS.index((da, 0))
                side_y = DIRECTIONS.index((0, db))
                around[to_x, to_y] = select(
                    put_corners[k - 4],
                    jnp.concatenate(
                        [
                            phases[i, j],
                            landing[layer, side_x],
                            landing[layer, side_y],
                            landing[layer, k],
                        ],
                        axis=0,
                    ),
                )

        for i in range(edge):
            total = totals[i]
            for shift_x in range(3):
                for shift_y in range(3):
                    if shift_y == 1 and 1 <= i + shift_x <= edge:
                        continue
                    window = around[i + shift_x, shift_y : shift_y + edge]
                    total = total + jnp.dot(
                        window.reshape(edge * blocks, every),
                        band_ref[layer * 9 + shift_x * 3 + shift_y],
                        preferred_element_type=jnp.float32,
                    )
            activated = (total / (1.0 + jnp.exp(-total))).astype(jnp.bfloat16)
            phases[i] = activated.reshape(edge, blocks, every)
            if layer == layers - 1:
                for j in range(edge):
                    cell = i * edge + j
                    values[:, :, cell * every : (cell + 1) * every] = select(
                        picks, phases[i, j]
                    ).reshape(values.shape[0], values.shape[1], every)
                for t in range(1, rows):
                    back(i, t).start()
                back_own(i).start()

    for t in range(1, rows):
        tell(t).wait_send()
        for i in range(edge):
            go(i, t).wait_send()
    for i in range(edge):
        back_own(i).wait()
        for t in range(1, rows):
            back(i, t).wait_recv()
        for j in range(edge):
            lanes = slice((i * edge + j) * every, (i * edge + j + 1) * every)
            out_ref[:, lanes] = lax.dot_general(
                send_picks[...],
                returned[:, :, lanes].reshape(queue, every),
                (((0,), (0,)), ((), ())),
                preferred_element_type=jnp.float32,
            ).astype(jnp.bfloat16)
    for i in range(edge):
        for t in range(1, rows):
            back(i, t).wait_send()
    for layer in range(layers):
        for k, (da, db) in enumerate(DIRECTIONS):

            @pl.when(present(da, db))
            def _():
                pltpu.make_async_remote_copy(
                    src_ref=leaving.at[layer, k],
                    dst_ref=landing.at[layer, k],
                    send_sem=send_sem.at[layer, k],
                    recv_sem=recv_sem.at[layer, k],
                    device_id=(me_column + db, me_row + da),
                    device_id_type=MESH,
                ).wait_send()


def exchange_and_convolve(sent_ids, send_picks, local_sums, w_conv):
    edge = BLOCK_EDGE_CELLS
    blocks = (TX // edge) * (TY // edge)
    layers, channels, outs = w_conv.shape[0], w_conv.shape[4], w_conv.shape[5]
    every = GZ * channels
    rows, per_owner = sent_ids.shape[:2]
    stacked = w_conv.reshape(layers * 9, 3 * channels, outs)
    selectors = halo_selectors()
    halo = (layers, len(DIRECTIONS), selectors[0].shape[1], every)
    queue = (rows, per_owner, edge * edge * every)
    return pl.pallas_call(
        functools.partial(conv_kernel, (lax.axis_size("grid"), lax.axis_size("pts"))),
        out_shape=jax.ShapeDtypeStruct(local_sums.shape, jnp.bfloat16),
        in_specs=[pl.BlockSpec(memory_space=pltpu.VMEM)] * 8,
        out_specs=pl.BlockSpec(memory_space=pltpu.VMEM),
        scratch_shapes=[
            pltpu.VMEM(sent_ids.shape, jnp.bfloat16),
            pltpu.VMEM(queue, jnp.bfloat16),
            pltpu.VMEM(queue, jnp.bfloat16),
            pltpu.VMEM(queue, jnp.bfloat16),
            pltpu.VMEM(queue, jnp.bfloat16),
            pltpu.VMEM((edge, edge * blocks, every), jnp.float32),
            pltpu.VMEM((layers * 9, every, every), jnp.bfloat16),
            pltpu.VMEM((edge, edge, blocks, every), jnp.bfloat16),
            pltpu.VMEM((edge + 2, edge + 2, blocks, every), jnp.bfloat16),
            pltpu.VMEM(halo, jnp.bfloat16),
            pltpu.VMEM(halo, jnp.bfloat16),
            pltpu.SemaphoreType.DMA(halo[:2]),
            pltpu.SemaphoreType.DMA(halo[:2]),
            pltpu.SemaphoreType.DMA((rows,)),
            pltpu.SemaphoreType.DMA((rows,)),
            pltpu.SemaphoreType.DMA((edge, rows)),
            pltpu.SemaphoreType.DMA((edge, rows)),
            pltpu.SemaphoreType.DMA((edge, rows)),
            pltpu.SemaphoreType.DMA((edge, rows)),
            pltpu.SemaphoreType.DMA((edge + 1,)),
        ],
        compiler_params=pltpu.CompilerParams(collective_id=0, has_side_effects=True),
    )(sent_ids, send_picks, local_sums, stacked, *selectors)


def per_device(
    features, w_in, w_mid, w_conv, point_frac, point_base, slot_dest, slot_tile_block, slot_count
):
    slot_total = slot_dest.shape[0]
    slot_width = features.shape[1] // slot_total
    owners = lax.axis_size("grid")
    per_owner = max(2, 2 * slot_total // owners)
    queue_length = owners * per_owner
    hidden_one = point_layer(w_in, features)
    hidden_two = point_layer(w_mid, hidden_one)
    channels = hidden_two.shape[0]
    hidden_two = hidden_two.reshape(channels, slot_total, slot_width)
    offsets, corners = lax.optimization_barrier(
        (
            point_frac.reshape(3, slot_total, slot_width),
            point_base.reshape(3, slot_total, slot_width),
        )
    )
    slot_order = jnp.arange(slot_total, dtype=jnp.int32)
    same_owner = (slot_dest[:, None] == slot_dest[None, :]) & (
        slot_order[None, :] < slot_order[:, None]
    )
    rank_within = jnp.sum(same_owner.astype(jnp.int32), axis=1)
    send_place = slot_dest * per_owner + rank_within
    send_match = send_place[None, :] == jnp.arange(queue_length, dtype=jnp.int32)[:, None]
    sent_block = jnp.sum(jnp.where(send_match, slot_tile_block[None, :] + 1, 0), axis=1) - 1
    send_picks = send_match.astype(jnp.bfloat16)
    weights = trilinear(offsets, corners, slot_count, BLOCK_EDGE_CELLS, GZ)
    local_sums = splat(weights, hidden_two).reshape(slot_total, -1)
    sent_ids = jnp.broadcast_to(sent_block[:, None], (queue_length, ID_LANES)).astype(jnp.bfloat16)
    blocks = exchange_and_convolve(
        sent_ids.reshape(owners, per_owner, ID_LANES), send_picks, local_sums, w_conv
    )
    interp = interpolate(weights, blocks)
    point_out = (hidden_two.astype(jnp.float32) + interp.astype(jnp.float32)).astype(jnp.bfloat16)
    return point_out.reshape(channels, slot_total * slot_width)


def solution(mesh):
    return jax.shard_map(
        per_device,
        mesh=mesh,
        in_specs=(
            P(None, ("pts", "grid")),
            P(),
            P(),
            P(),
            P(None, ("pts", "grid")),
            P(None, ("pts", "grid")),
            P(("pts", "grid")),
            P(("pts", "grid")),
            P(("pts", "grid")),
        ),
        out_specs=P(None, ("pts", "grid")),
        check_vma=False,
    )
```

profile of v0, /device:TPU:0, one launch (start us, length us, event | category | flops | bytes accessed | tf_op | source)
XLA Modules:
  0.0 141.8 jit_solution(12044854318541594632)
XLA Ops:
  0.0 1.1 copy.42
  1.1 0.0 copy-start.7
  1.1 1.0 copy.43
  2.2 1.5 %add_multiply_fusion = f32[16,64,256]{2,0,1:T(8,128)} fusion(f32[64,256]{1,0:T(8,128)S(1)} %get-tuple-element.17, s32[64,256]{1,0:T(8,128)S(1)} %get-tuple-element.11, f32[64,256]{1,0:T(8,128)S(1)} %get-tuple-element.20, s32[64,256]{1,0:T(8,128)S(1)} %get-tuple-element.14, f32[64,256]{1,0:T(8,128)S(1)} %get-tuple-element.16, ...), kind=kLoop, calls=%fused_computation.18 | loop fusion | flops 2883584 | bytes 1572992 | tf_op jit(solution)/shard_map/mul | solution.py:43
  3.7 0.9 select_add_fusion
  4.7 2.7 %multiply_convert_fusion.3 = bf16[64,16384]{1,0:T(8,128)(2,1)S(1)} fusion(bf16[64,64]{1,0:T(8,128)(2,1)S(1)} %copy-done.7, bf16[32,64]{1,0:T(8,128)(2,1)S(1)} %copy-done.8, bf16[32,16384]{1,0:T(8,128)(2,1)S(1)} %copy-done), kind=kOutput, calls=%fused_computation.13 | convolution fusion | flops 211812352 | bytes 3158016 | tf_op jit(solution)/shard_map/dot_general | solution.py:21
  7.3 0.0 copy-start.1
  7.4 0.5 copy.34
  7.9 0.7 copy-done.1
  8.7 0.1 fusion.15
  8.7 0.6 copy-done.2
  9.4 0.1 copy-done.3
  9.5 3.3 %fusion.11 = bf16[64,16,8,64]{3,2,1,0:T(8,128)(2,1)S(1)} fusion(bf16[64,64,256,1]{2,1,0,3:T(8,128)(2,1)S(1)} %bitcast.68, f32[64,256]{1,0:T(8,128)S(1)} %fusion.15, f32[8,64,256]{2,0,1:T(8,128)S(1)} %copy-done.3, f32[16,64,256]{2,0,1:T(8,128)S(1)} %copy-done.2), kind=kOutput, calls=%fused_computation.17 | convolution fusion | flops 275251200 | bytes 4784128 | tf_op jit(solution)/shard_map/czsp,hsp->sczh/dot_general | solution.py:48
  12.8 0.0 copy-start.6
  12.8 2.5 %reshape_reshape.3.sums_ref = bf16[64,8192]{1,0:T(8,128)(2,1)} reshape(bf16[64,16,8,64]{3,2,1,0:T(8,128)(2,1)S(1)} %fusion.11) | data formatting | bytes 2097152 | tf_op jit(solution)/shard_map/reshape;reshape | solution.py:484
  15.3 0.2 convert_reduce_fusion
  15.5 0.1 select_reduce_fusion
  15.6 0.1 convert_element_type.54
  15.7 0.7 broadcast_in_dim.95.ids_ref
  16.4 0.6 fusion.14.send_picks
  17.0 117.0 %shard_map.127 = bf16[64,8192]{1,0:T(8,128)(2,1)} custom-call(bf16[8,16,128]{2,1,0:T(8,128)(2,1)} %broadcast_in_dim.95.ids_ref, bf16[128,64]{1,0:T(8,128)(2,1)} %fusion.14.send_picks, bf16[64,8192]{1,0:T(8,128)(2,1)} %reshape_reshape.3.sums_ref, bf16[18,192,64]{2,1,0:T(8,128)(2,1)} %bitcast.69, bf16[4,32,256]{2,1,0:T(8,128)(2,1)} %constant.53.clone.cut_sides, ...), custom_call_target="tpu_custom_call" | custom-call | tf_op jit(solution)/shard_map/pallas_call | solution.py:425
  134.1 3.3 %reshape.100 = bf16[64,16,8,64]{3,2,1,0:T(8,128)(2,1)S(1)} reshape(bf16[64,8192]{1,0:T(8,128)(2,1)} %shard_map.127) | data formatting | bytes 2097152 | tf_op jit(solution)/shard_map/reshape | solution.py:53
  137.3 3.0 %fusion.9 = bf16[64,8,8,256]{3,2,1,0:T(8,128)(2,1)S(1)} fusion(bf16[8,64,8,256]{3,2,1,0:T(8,128)(2,1)} %bitcast.67, bf16[64,16,8,64]{3,2,1,0:T(8,128)(2,1)S(1)} %reshape.100, f32[64,256]{1,0:T(8,128)S(1)} %fusion.15, f32[8,64,256]{2,0,1:T(8,128)} %select_add_fusion, f32[16,64,256]{2,0,1:T(8,128)} %add_multiply_fusion), kind=kOutput, calls=%fused_computation.15 | convolution fusion | flops 279969792 | bytes 6881280 | tf_op jit(solution)/shard_map/czsp,sczh->hsp/dot_general | solution.py:54
  140.3 1.5 %copy.31 = bf16[64,8,8,256]{3,2,0,1:T(8,128)(2,1)} copy(bf16[64,8,8,256]{3,2,1,0:T(8,128)(2,1)S(1)} %fusion.9) | data formatting | bytes 4194304 | tf_op jit(solution)/shard_map/reshape | solution.py:491
  (17 shorter events, 0.1 us)
Async XLA Ops:
  0.0 4.7 %copy-start = (bf16[32,16384]{1,0:T(8,128)(2,1)S(1)}, bf16[32,16384]{1,0:T(8,128)(2,1)}, u32[]{:S(2)}) copy-start(bf16[32,16384]{1,0:T(8,128)(2,1)} %param.13) | copy-start | bytes 3145732
  1.1 3.6 %copy-start.7 = (bf16[64,64]{1,0:T(8,128)(2,1)S(1)}, bf16[64,64]{1,0:T(8,128)(2,1)}, u32[]{:S(2)}) copy-start(bf16[64,64]{1,0:T(8,128)(2,1)} %param.15) | copy-start | bytes 24580
  1.1 3.6 %copy-start.8 = (bf16[32,64]{1,0:T(8,128)(2,1)S(1)}, bf16[32,64]{1,0:T(8,128)(2,1)}, u32[]{:S(2)}) copy-start(bf16[32,64]{1,0:T(8,128)(2,1)} %param.14) | copy-start | bytes 12292
  7.3 1.3 copy-start.1
  7.4 1.3 copy-start.4
  7.4 2.0 %copy-start.2 = (f32[16,64,256]{2,0,1:T(8,128)S(1)}, f32[16,64,256]{2,0,1:T(8,128)}, u32[]{:S(2)}) copy-start(f32[16,64,256]{2,0,1:T(8,128)} %add_multiply_fusion) | copy-start | bytes 3145732
  7.4 2.1 %copy-start.3 = (f32[8,64,256]{2,0,1:T(8,128)S(1)}, f32[8,64,256]{2,0,1:T(8,128)}, u32[]{:S(2)}) copy-start(f32[8,64,256]{2,0,1:T(8,128)} %select_add_fusion) | copy-start | bytes 1572868
  12.8 2.5 %copy-start.5 = (s32[64]{0:T(128)S(1)}, s32[64]{0:T(128)}, u32[]{:S(2)}) copy-start(s32[64]{0:T(128)} %param.19) | copy-start | bytes 772
  12.8 2.7 %copy-start.6 = (s32[64]{0:T(128)S(1)}, s32[64]{0:T(128)}, u32[]{:S(2)}) copy-start(s32[64]{0:T(128)} %param.20) | copy-start | bytes 772
where the time goes:
time: 143 us; the launch traced here: 142 us
  Pallas kernels  117 us (82%)
  local copies, waits for them, and re-layouts  12.1 us (8%)
  matrix products  8.94 us (6%)
  other arithmetic  3.51 us (2%)
    pallas_call x1, Pallas kernels, exchange_and_convolve(): pl.pallas_call(functools.partial(conv_kernel, (lax.axis_size('grid'), lax...  117 us
    unnamed x21, local copies, waits for them, and re-layouts  4.14 us
    dot_general x1, matrix products, splat(): jnp.einsum('czsp,hsp->sczh', weights, hidden, preferred_element_type=jnp....  3.27 us
    reshape x1, local copies, waits for them, and re-layouts, interpolate(): blocks.reshape(blocks.shape[0], weights.shape[0], weights.shape[1], -1)  3.26 us
    dot_general x1, matrix products, interpolate(): jnp.einsum('czsp,sczh->hsp', weights, cells, preferred_element_type=jnp.f...  2.99 us

commit v1 on v0

v1 whole, which is shorter than its diff:
```python
import functools

import jax
import jax.numpy as jnp
from jax import lax
from jax.experimental import pallas as pl
from jax.experimental.pallas import tpu as pltpu
from jax.sharding import PartitionSpec as P

GZ = 8
EDGE = 4
TX = 32
TY = 32
LANES = 128
PAIR = 2
Z = GZ // PAIR
MESH = pl.DeviceIdType.MESH
DIRECTIONS = ((0, 1), (0, -1), (1, 0), (-1, 0), (1, 1), (1, -1), (-1, 1), (-1, -1))
ORDER = (3, 0, 1, 2)
OUT_ORDER = (0, 3, 1, 2)


def point_layer(weight, inputs):
    mixed_sum = lax.dot_general(
        weight, inputs, (((0,), (0,)), ((), ())), preferred_element_type=jnp.float32
    )
    return jax.nn.silu(mixed_sum).astype(jnp.bfloat16)


def axis_weights(offset, corner, positions):
    positions = positions[:, None, None]
    below_part = jnp.where(positions == corner[None], 1.0 - offset[None], 0.0)
    above_part = jnp.where(positions == corner[None] + 1, offset[None], 0.0)
    return below_part + above_part


def trilinear(offsets, corners, counts, block_edge, grid_depth):
    slot_width = offsets.shape[2]
    live_mask = (jnp.arange(slot_width, dtype=jnp.int32)[None, :] < counts[:, None]).astype(
        jnp.float32
    )
    cells = jnp.arange(block_edge * block_edge, dtype=jnp.int32)
    along_x = axis_weights(offsets[0], corners[0], cells // block_edge)
    along_y = axis_weights(offsets[1], corners[1], cells % block_edge)
    along_z = axis_weights(offsets[2], corners[2], jnp.arange(grid_depth, dtype=jnp.int32))
    corner_weights = (along_x * along_y)[:, None] * along_z[None] * live_mask
    return corner_weights.astype(jnp.bfloat16)


def splat(weights, hidden):
    sums = jnp.einsum("czsp,hsp->sczh", weights, hidden, preferred_element_type=jnp.float32)
    slots, channels = sums.shape[0], sums.shape[3]
    sums = sums.astype(jnp.bfloat16)
    sums = sums.reshape(slots, EDGE, EDGE // PAIR, PAIR, Z, PAIR, channels)
    sums = sums.transpose(4, 1, 0, 2, 5, 3, 6)
    return sums.reshape(Z, EDGE, slots, EDGE * PAIR * channels)


def interpolate(weights, blocks):
    slots, channels = blocks.shape[2], blocks.shape[3] // (EDGE * PAIR)
    cells = blocks.reshape(Z, EDGE, slots, EDGE // PAIR, PAIR, PAIR, channels)
    cells = cells.transpose(2, 1, 3, 5, 0, 4, 6).reshape(slots, EDGE * EDGE, GZ, channels)
    return jnp.einsum("czsp,sczh->hsp", weights, cells, preferred_element_type=jnp.float32).astype(
        jnp.bfloat16
    )


def build_band(w_ref, band_ref):
    channels = w_ref.shape[1]
    width = PAIR * channels

    def one(n, carry):
        layer, a = lax.div(n, 3), lax.rem(n, 3)
        band_ref[layer, :, a] = jnp.zeros(band_ref.shape[1:2] + band_ref.shape[3:], band_ref.dtype)
        for zl in range(2 + PAIR):
            part, slot = (0, zl - 1) if 1 <= zl <= PAIR else (1, 0 if zl == 0 else 1)
            for zz in range(PAIR):
                e = zl - zz
                if not 0 <= e <= 2:
                    continue
                for source, row in ((0, 0), (1, 1), (2, 2), (-1, 3)):
                    for target in range(PAIR):
                        b = source - target + 1
                        if not 0 <= b <= 2:
                            continue
                        rows = slice(row * channels, (row + 1) * channels)
                        lanes = zz * width + target * channels
                        band_ref[layer, part, a, slot, rows, lanes : lanes + channels] = w_ref[
                            n * 9 + b * 3 + e
                        ]
        return carry

    lax.fori_loop(0, band_ref.shape[0] * 3, one, 0)


def conv_kernel(
    sizes,
    ids_ref,
    sums_ref,
    w_ref,
    out_ref,
    ids,
    arrived,
    field,
    band_ref,
    totals,
    sum_picks,
    out_picks,
    dense,
    values,
    id_send,
    id_recv,
    z_send,
    z_recv,
    x_send,
    x_recv,
    halo_send,
    halo_recv,
    rx_send,
    rx_recv,
    rz_send,
    rz_recv,
):
    rows, columns = sizes
    strips = rows // Z
    blocks = dense.shape[2]
    slots = ids.shape[1]
    span = (field.shape[4] - blocks) // 2
    layers = field.shape[0]
    me_row, me_column = lax.axis_index("grid"), lax.axis_index("pts")
    me_z, me_x = lax.div(me_row, strips), lax.rem(me_row, strips)
    inner = pl.ds(span, blocks)

    def place(dz, ds):
        strip = me_column * strips + me_x + ds
        z = me_z + dz
        present = (strip >= 0) & (strip < columns * strips) & (z >= 0) & (z < Z)
        column = lax.div(strip + strips, strips) - 1
        return present, column, z * strips + lax.rem(strip + strips, strips)

    def tell(t):
        return pltpu.make_async_remote_copy(
            src_ref=ids_ref,
            dst_ref=ids.at[me_row],
            send_sem=id_send.at[t],
            recv_sem=id_recv.at[t],
            device_id=(me_column, lax.rem(me_row + t, rows)),
            device_id_type=MESH,
        )

    def along_z(i, t):
        z = lax.rem(me_z + t, Z)
        return pltpu.make_async_remote_copy(
            src_ref=sums_ref.at[z, i],
            dst_ref=arrived.at[i, me_row],
            send_sem=z_send.at[i, t],
            recv_sem=z_recv.at[i, t],
            device_id=(me_column, z * strips + me_x),
            device_id_type=MESH,
        )

    def along_x(i, t, u):
        origin = lax.rem(me_z - t + Z, Z) * strips + me_x
        return pltpu.make_async_remote_copy(
            src_ref=sums_ref.at[me_z, i] if t == 0 else arrived.at[i, origin],
            dst_ref=arrived.at[i, origin],
            send_sem=x_send.at[i, t, u],
            recv_sem=x_recv.at[i, t, u],
            device_id=(me_column, me_z * strips + lax.rem(me_x + u, strips)),
            device_id_type=MESH,
        )

    def halo(layer, i, k):
        dz, ds = DIRECTIONS[k]
        _, column, row = place(dz, ds)
        pairs = slice(0, PAIR) if ds == 0 else slice(1, 2) if ds > 0 else slice(0, 1)
        source_z = slice(1, 3) if dz == 0 else slice(2, 3) if dz > 0 else slice(1, 2)
        target_z = slice(1, 3) if dz == 0 else slice(0, 1) if dz > 0 else slice(3, 4)
        if ds == 0:
            source_rows = target_rows = slice(span, span + blocks)
        elif ds > 0:
            source_rows, target_rows = slice(blocks, blocks + span), slice(0, span)
        else:
            source_rows = slice(span, 2 * span)
            target_rows = slice(span + blocks, 2 * span + blocks)
        return pltpu.make_async_remote_copy(
            src_ref=field.at[layer, i + 1, pairs, source_z, source_rows],
            dst_ref=field.at[layer, i + 1, pairs, target_z, target_rows],
            send_sem=halo_send.at[layer, i, k],
            recv_sem=halo_recv.at[layer, i, k],
            device_id=(column, row),
            device_id_type=MESH,
        )

    def back_x(i, u):
        return pltpu.make_async_remote_copy(
            src_ref=dense.at[i, me_x],
            dst_ref=dense.at[i, me_x],
            send_sem=rx_send.at[i, u],
            recv_sem=rx_recv.at[i, u],
            device_id=(me_column, me_z * strips + lax.rem(me_x + u, strips)),
            device_id_type=MESH,
        )

    def back_z(i, t):
        z = lax.rem(me_z + t, Z)
        return pltpu.make_async_remote_copy(
            src_ref=values.at[i, z],
            dst_ref=out_ref.at[me_z, i],
            send_sem=rz_send.at[i, t],
            recv_sem=rz_recv.at[i, t],
            device_id=(me_column, z * strips + me_x),
            device_id_type=MESH,
        )

    def send_halos(layer, i):
        for k, (dz, ds) in enumerate(DIRECTIONS):
            present, _, _ = place(dz, ds)

            @pl.when(present)
            def _():
                halo(layer, i, k).start()

    def wait_halos(layer, i, ks):
        for k in ks:
            dz, ds = DIRECTIONS[k]
            present, _, _ = place(-dz, -ds)

            @pl.when(present)
            def _():
                halo(layer, i, k).wait_recv()

    barrier = pltpu.get_barrier_semaphore()
    for t in range(1, rows):
        pl.semaphore_signal(
            barrier,
            inc=1,
            device_id=(me_column, lax.rem(me_row + t, rows)),
            device_id_type=MESH,
        )
    expected = rows - 1
    for dz in (-1, 0, 1):
        for ds in (-1, 1):
            present, column, row = place(dz, ds)
            other = present & (column != me_column)
            expected = expected + other.astype(jnp.int32)

            @pl.when(other)
            def _():
                pl.semaphore_signal(barrier, inc=1, device_id=(column, row), device_id_type=MESH)

    pl.semaphore_wait(barrier, expected)

    for t in range(1, rows):
        tell(t).start()
    for i in ORDER:
        for t in (2, 1, 3):
            along_z(i, t).start()
        for u in range(1, strips):
            along_x(i, 0, u).start()
    for i in ORDER:
        arrived[i, me_row] = sums_ref[me_z, i]
    ids[me_row] = ids_ref[...]
    for k, (dz, ds) in enumerate(DIRECTIONS):
        present, _, _ = place(-dz, -ds)

        @pl.when(jnp.logical_not(present))
        def _():
            target_z = slice(1, 3) if dz == 0 else slice(0, 1) if dz > 0 else slice(3, 4)
            pairs = slice(0, PAIR) if ds == 0 else slice(1, 2) if ds > 0 else slice(0, 1)
            low, high = (
                (span, span + blocks)
                if ds == 0
                else (0, span)
                if ds > 0
                else (span + blocks, 2 * span + blocks)
            )
            for layer in range(layers):
                view = field.at[layer, 1 : EDGE + 1, pairs, target_z, low:high]
                view[...] = jnp.zeros(view.shape, field.dtype)

    build_band(w_ref, band_ref)
    for t in range(1, rows):
        tell(t).wait_recv()

    def picks(named, first, width):
        parts = []
        for low in range(0, width, LANES):
            place_of = lax.broadcasted_iota(jnp.int32, named.shape, 1) + (low + first)
            parts.append(jnp.where(named == place_of, 1.0, 0.0))
        return jnp.concatenate(parts, axis=1)

    for r in range(rows):
        one_hot = picks(ids[r], me_x * blocks, blocks)
        sum_picks[:, r * slots : (r + 1) * slots] = one_hot.T.astype(jnp.bfloat16)
    for z in range(Z):
        out_picks[z * slots : (z + 1) * slots] = picks(
            ids[z * strips + me_x], 0, strips * blocks
        ).astype(jnp.bfloat16)

    def forward(i):
        for t in (1, 2, 3):
            along_z(i, t).wait_recv()
            for u in range(1, strips):
                along_x(i, t, u).start()

    def spread(layer, i, tiles):
        for jp in range(PAIR):
            for zz in range(PAIR):
                field[layer, i + 1, jp, 1 + zz, inner] = tiles(jp, zz)
        send_halos(layer, i)

    def gather(i):
        for t in range(Z):
            for u in range(1, strips):
                along_x(i, t, u).wait_recv()
        summed = jnp.dot(
            sum_picks[...],
            arrived[i].reshape(rows * slots, arrived.shape[3]),
            preferred_element_type=jnp.float32,
        ).astype(jnp.bfloat16)

        def tiles(jp, zz):
            low = (jp * PAIR + zz) * LANES
            return summed[:, low : low + LANES]

        spread(0, i, tiles)

    for n, i in enumerate(ORDER):
        forward(i)
        if n > 0:
            gather(ORDER[n - 1])
    gather(ORDER[-1])

    low_half = lax.broadcasted_iota(jnp.int32, (blocks, LANES), 1) < LANES // PAIR

    def shift(layer, down, levels):
        source, target = (EDGE, 0) if down else (1, EDGE + 1)
        for jp in range(PAIR):
            low = 0 if jp == 1 else span
            size = blocks + span
            ranks = lax.broadcasted_iota(jnp.int32, (size, LANES), 0)
            edge_rank = 0 if down else span - 1
            keep = lax.rem(ranks, span) != edge_rank
            for zl in levels:
                moved = pltpu.roll(
                    field[layer, source, jp, zl, low : low + size].astype(jnp.float32),
                    1 if down else size - 1,
                    0,
                )
                field[layer, target, jp, zl, low : low + size] = jnp.where(
                    keep, moved, 0.0
                ).astype(jnp.bfloat16)

    def windows(layer, i, jp, levels):
        parts = []
        for a in range(3):
            for zl in levels:
                here = field.at[layer, i + a, :, zl]
                parts.append(here[jp, inner])
                if jp == 0:
                    up, down = here[1, inner], here[1, 0:blocks]
                else:
                    up, down = here[0, 2 * span : 2 * span + blocks], here[0, inner]
                parts.append(jnp.where(low_half, up, down))
        return jnp.concatenate(parts, axis=1)

    def conv_terms(layer, i, part):
        levels = (1, 2) if part == 0 else (0, 3)
        weight = band_ref[layer, part].reshape(-1, band_ref.shape[5])
        lhs = jnp.concatenate([windows(layer, i, jp, levels) for jp in range(PAIR)], axis=0)
        return jnp.dot(lhs, weight, preferred_element_type=jnp.float32)

    beside = [k for k, (dz, _) in enumerate(DIRECTIONS) if dz == 0]
    across = [k for k, (dz, _) in enumerate(DIRECTIONS) if dz != 0]
    for layer in range(layers):
        before = ORDER if layer == 0 else OUT_ORDER
        for i in before:
            wait_halos(layer, i, beside)
        shift(layer, True, (1, 2))
        shift(layer, False, (1, 2))
        for i in OUT_ORDER:
            totals[i] = conv_terms(layer, i, 0)
        waited = set()
        for i in OUT_ORDER:
            needed = {(i - 1) % EDGE, i, (i + 1) % EDGE}
            for phase in before:
                if phase in needed and phase not in waited:
                    wait_halos(layer, phase, across)
                    waited.add(phase)
                    if phase == EDGE - 1:
                        shift(layer, True, (0, 3))
                    if phase == 0:
                        shift(layer, False, (0, 3))
            total = totals[i] + conv_terms(layer, i, 1)
            activated = (total / (1.0 + jnp.exp(-total))).astype(jnp.bfloat16)

            def tiles(jp, zz):
                return activated[
                    jp * blocks : (jp + 1) * blocks, zz * LANES : (zz + 1) * LANES
                ]

            if layer < layers - 1:
                spread(layer + 1, i, tiles)
            else:
                for jp in range(PAIR):
                    for zz in range(PAIR):
                        low = (jp * PAIR + zz) * LANES
                        dense[i, me_x, :, low : low + LANES] = tiles(jp, zz)
                for u in range(1, strips):
                    back_x(i, u).start()

    for i in OUT_ORDER:
        for u in range(1, strips):
            back_x(i, u).wait_recv()
        picked = jnp.dot(
            out_picks[...],
            dense[i].reshape(strips * blocks, dense.shape[3]),
            preferred_element_type=jnp.float32,
        ).astype(jnp.bfloat16)
        values[i] = picked.reshape(values.shape[1:])
        for t in (2, 1, 3):
            back_z(i, t).start()
        out_ref[me_z, i] = values[i, me_z]

    for t in range(1, rows):
        tell(t).wait_send()
    for i in range(EDGE):
        for t in (1, 2, 3):
            back_z(i, t).wait_recv()
            back_z(i, t).wait_send()
            along_z(i, t).wait_send()
        for u in range(1, strips):
            back_x(i, u).wait_send()
            for t in range(Z):
                along_x(i, t, u).wait_send()
        for layer in range(layers):
            for k, (dz, ds) in enumerate(DIRECTIONS):
                present, _, _ = place(dz, ds)

                @pl.when(present)
                def _():
                    halo(layer, i, k).wait_send()


def exchange_and_convolve(ids, sums, w_conv):
    rows, columns = lax.axis_size("grid"), lax.axis_size("pts")
    strips = rows // Z
    slots, width = sums.shape[2:]
    layers, channels = w_conv.shape[0], w_conv.shape[4]
    span = rows * (TX // EDGE)
    blocks = span * (TY // EDGE) // strips
    halos = (layers, EDGE, len(DIRECTIONS))
    dma = pltpu.SemaphoreType.DMA
    return pl.pallas_call(
        functools.partial(conv_kernel, (rows, columns)),
        out_shape=jax.ShapeDtypeStruct(sums.shape, jnp.bfloat16),
        in_specs=[pl.BlockSpec(memory_space=pltpu.VMEM)] * 3,
        out_specs=pl.BlockSpec(memory_space=pltpu.VMEM),
        scratch_shapes=[
            pltpu.VMEM((rows, slots, LANES), jnp.int32),
            pltpu.VMEM((EDGE, rows, slots, width), jnp.bfloat16),
            pltpu.VMEM((layers, EDGE + 2, PAIR, PAIR + 2, blocks + 2 * span, LANES), jnp.bfloat16),
            pltpu.VMEM((layers, 2, 3, 2, 2 * LANES, 2 * LANES), jnp.bfloat16),
            pltpu.VMEM((EDGE, PAIR * blocks, 2 * LANES), jnp.float32),
            pltpu.VMEM((blocks, rows * slots), jnp.bfloat16),
            pltpu.VMEM((Z * slots, strips * blocks), jnp.bfloat16),
            pltpu.VMEM((EDGE, strips, blocks, width), jnp.bfloat16),
            pltpu.VMEM((EDGE, Z, slots, width), jnp.bfloat16),
            dma((rows,)),
            dma((rows,)),
            dma((EDGE, Z)),
            dma((EDGE, Z)),
            dma((EDGE, Z, strips)),
            dma((EDGE, Z, strips)),
            dma(halos),
            dma(halos),
            dma((EDGE, strips)),
            dma((EDGE, strips)),
            dma((EDGE, Z)),
            dma((EDGE, Z)),
        ],
        compiler_params=pltpu.CompilerParams(collective_id=0, has_side_effects=True),
    )(ids, sums, w_conv.reshape(layers * 27, channels, channels))


def per_device(
    features, w_in, w_mid, w_conv, point_frac, point_base, slot_dest, slot_tile_block, slot_count
):
    slot_total = slot_dest.shape[0]
    slot_width = features.shape[1] // slot_total
    span = lax.axis_size("grid") * (TX // EDGE)
    along, across = TX // EDGE, TY // EDGE
    hidden_one = point_layer(w_in, features)
    hidden_two = point_layer(w_mid, hidden_one)
    channels = hidden_two.shape[0]
    hidden_two = hidden_two.reshape(channels, slot_total, slot_width)
    offsets, corners = lax.optimization_barrier(
        (
            point_frac.reshape(3, slot_total, slot_width),
            point_base.reshape(3, slot_total, slot_width),
        )
    )
    block_x = slot_dest * along + slot_tile_block // across
    block_y = slot_tile_block % across
    ids = jnp.broadcast_to((block_y * span + block_x)[:, None], (slot_total, LANES))
    weights = trilinear(offsets, corners, slot_count, EDGE, GZ)
    local_sums = splat(weights, hidden_two)
    blocks = exchange_and_convolve(ids, local_sums, w_conv)
    interp = interpolate(weights, blocks)
    point_out = (hidden_two.astype(jnp.float32) + interp.astype(jnp.float32)).astype(jnp.bfloat16)
    return point_out.reshape(channels, slot_total * slot_width)


def solution(mesh):
    return jax.shard_map(
        per_device,
        mesh=mesh,
        in_specs=(
            P(None, ("pts", "grid")),
            P(),
            P(),
            P(),
            P(None, ("pts", "grid")),
            P(None, ("pts", "grid")),
            P(("pts", "grid")),
            P(("pts", "grid")),
            P(("pts", "grid")),
        ),
        out_specs=P(None, ("pts", "grid")),
        check_vma=False,
    )
```

time: 143 us -> 139 us (0.972)
  Pallas kernels: 117 us -> 107 us
  local copies, waits for them, and re-layouts: 12.1 us -> 19.3 us
  matrix products: 8.94 us -> 6.67 us
  other arithmetic: 3.51 us -> 4.94 us
    pallas_call x1, Pallas kernels: 117 us -> 107 us  [exchange_and_convolve(): pl.pallas_call(functools.partial(conv_kernel, (rows, columns)), out_shape...]
    reshape x1 -> x3, local copies, waits for them, and re-layouts: 3.26 us -> 8.86 us  [the longest x1 4.65 us: interpolate(): cells = blocks.reshape(Z, EDGE, slots, EDGE // PAIR, PAIR, PAIR, channels)]
    convert_element_type x2 -> x1, other arithmetic: 0.63 us -> 4.09 us  [trilinear(): return corner_weights.astype(jnp.bfloat16)]
    another operation x1 -> x0, local copies, waits for them, and re-layouts: 2.49 us -> none  [per_device(): local_sums = splat(weights, hidden_two).reshape(slot_total, -1)]
    transpose x0 -> x1, local copies, waits for them, and re-layouts: none -> 2.29 us  [interpolate(): cells.transpose(2, 1, 3, 5, 0, 4, 6)]
    unnamed x21 -> x29, local copies, waits for them, and re-layouts: 4.14 us -> 6.01 us
    dot_general x1, matrix products: 2.99 us -> 1.41 us  [interpolate(): jnp.einsum('czsp,sczh->hsp', weights, cells, preferred_element_type=jnp.f...]
where the time goes in v1:
time: 139 us; the launch traced here: 138 us
  Pallas kernels  107 us (77%)
  local copies, waits for them, and re-layouts  19.3 us (14%)
  matrix products  6.67 us (5%)
  other arithmetic  4.94 us (4%)
    pallas_call x1, Pallas kernels, exchange_and_convolve(): pl.pallas_call(functools.partial(conv_kernel, (rows, columns)), out_shape...  107 us
    unnamed x29, local copies, waits for them, and re-layouts  6.01 us
    reshape x1, local copies, waits for them, and re-layouts, interpolate(): cells = blocks.reshape(Z, EDGE, slots, EDGE // PAIR, PAIR, PAIR, channels)  4.65 us
    convert_element_type x1, other arithmetic, trilinear(): return corner_weights.astype(jnp.bfloat16)  4.09 us

profile of v1, /device:TPU:0, one launch (start us, length us, event | category | flops | bytes accessed | tf_op | source)
XLA Modules:
  0.0 137.9 jit_solution(9292239961058267816)
XLA Ops:
  0.0 1.1 copy.43
  1.1 1.0 copy.44
  2.2 0.0 copy-start.9
  2.2 0.0 copy-start.10
  2.2 0.6 add_multiply_fusion
  2.8 0.1 select_add_fusion
  3.0 0.1 fusion.10
  3.0 0.7 copy-done.2
  3.7 0.2 copy-done.4
  4.0 4.1 %multiply_convert_fusion = bf16[16,8,64,256]{3,0,1,2:T(8,128)(2,1)} fusion(f32[64,256]{1,0:T(8,128)S(1)} %fusion.10, f32[8,64,256]{2,0,1:T(8,128)S(1)} %select_add_fusion, f32[16,64,256]{2,0,1:T(8,128)S(1)} %add_multiply_fusion), kind=kLoop, calls=%fused_computation.1 | loop fusion | flops 6291456 | bytes 5832704 | tf_op jit(solution)/shard_map/convert_element_type | solution.py:47
  8.1 2.7 %multiply_convert_fusion.1 = bf16[64,16384]{1,0:T(8,128)(2,1)S(1)} fusion(bf16[64,64]{1,0:T(8,128)(2,1)S(1)} %copy-done.9, bf16[32,64]{1,0:T(8,128)(2,1)S(1)} %copy-done.10, bf16[32,16384]{1,0:T(8,128)(2,1)S(1)} %copy-done), kind=kOutput, calls=%fused_computation.7 | convolution fusion | flops 211812352 | bytes 3158016 | tf_op jit(solution)/shard_map/dot_general | solution.py:24
  10.7 0.0 copy-start.6
  10.8 0.5 copy.29
  11.3 2.4 %copy-done.1 = bf16[16,8,64,256]{3,0,1,2:T(8,128)(2,1)S(1)} copy-done((bf16[16,8,64,256]{3,0,1,2:T(8,128)(2,1)S(1)}, bf16[16,8,64,256]{3,0,1,2:T(8,128)(2,1)}, u32[]{:S(2)}) %copy-start.1) | copy-done | bytes 4194328
  13.7 2.6 %fusion.5 = bf16[64,16,8,64]{3,2,1,0:T(8,128)(2,1)S(1)} fusion(bf16[64,64,256,1]{2,1,0,3:T(8,128)(2,1)S(1)} %bitcast.76, bf16[16,8,64,256]{3,0,1,2:T(8,128)(2,1)S(1)} %copy-done.1), kind=kOutput, calls=%fused_computation.12 | convolution fusion | flops 268959744 | bytes 7340032 | tf_op jit(solution)/shard_map/czsp,hsp->sczh/dot_general | solution.py:51
  16.3 2.2 %copy.42 = bf16[64,4,2,2,4,2,64]{6,3,5,2,0,1,4:T(2,128)(2,1)S(1)} copy(bf16[64,4,2,2,4,2,64]{6,5,4,3,2,1,0:T(2,128)(2,1)S(1)} %bitcast.75) | data formatting | bytes 2097152 | tf_op jit(solution)/shard_map/reshape | solution.py:54
  18.5 2.1 %reshape.93.sums_ref = bf16[4,4,64,512]{3,2,1,0:T(8,128)(2,1)} reshape(bf16[4,4,64,2,2,2,64]{6,5,4,3,2,1,0:T(2,128)(2,1)S(1)} %bitcast.70) | data formatting | bytes 2097152 | tf_op jit(solution)/shard_map/reshape | solution.py:56
  20.6 0.7 broadcast_in_dim.74.ids_ref
  21.2 106.8 %shard_map.91 = bf16[4,4,64,512]{3,2,1,0:T(8,128)(2,1)} custom-call(s32[64,128]{1,0:T(8,128)} %broadcast_in_dim.74.ids_ref, bf16[4,4,64,512]{3,2,1,0:T(8,128)(2,1)} %reshape.93.sums_ref, bf16[54,64,64]{2,1,0:T(8,128)(2,1)} %bitcast.77), custom_call_target="tpu_custom_call" | custom-call | tf_op jit(solution)/shard_map/pallas_call | solution.py:455
  128.0 4.7 %reshape.95 = bf16[4,4,64,2,2,2,64]{6,5,4,3,2,1,0:T(2,128)(2,1)S(1)} reshape(bf16[4,4,64,512]{3,2,1,0:T(8,128)(2,1)} %shard_map.91) | data formatting | bytes 2097152 | tf_op jit(solution)/shard_map/reshape | solution.py:61
  132.7 0.0 copy-start.7
  132.7 2.3 %copy.19 = bf16[64,4,2,2,4,2,64]{6,3,2,1,5,4,0:T(2,128)(2,1)S(1)} copy(bf16[64,4,2,2,4,2,64]{6,3,5,2,0,1,4:T(2,128)(2,1)S(1)} %bitcast.71) | data formatting | bytes 2097152 | tf_op jit(solution)/shard_map/transpose | solution.py:62
  135.0 1.4 %fusion.3 = bf16[64,8,8,256]{3,2,1,0:T(8,128)(2,1)S(1)} fusion(bf16[8,64,8,256]{3,2,1,0:T(8,128)(2,1)S(1)} %bitcast.73, bf16[64,16,8,64]{3,1,2,0:T(8,128)(2,1)S(1)} %bitcast.74, f32[64,256]{1,0:T(8,128)S(1)} %fusion.10, f32[8,64,256]{2,0,1:T(8,128)S(1)} %copy-done.5, f32[16,64,256]{2,0,1:T(8,128)S(1)} %copy-done.3), kind=kOutput, calls=%fused_computation.9 | convolution fusion | flops 279969792 | bytes 6881280 | tf_op jit(solution)/shard_map/czsp,sczh->hsp/dot_general | solution.py:63
  136.5 1.5 %copy.26 = bf16[64,8,8,256]{3,2,0,1:T(8,128)(2,1)} copy(bf16[64,8,8,256]{3,2,1,0:T(8,128)(2,1)S(1)} %fusion.3) | data formatting | bytes 4194304 | tf_op jit(solution)/shard_map/reshape | solution.py:512
  (23 shorter events, 0.1 us)
Async XLA Ops:
  0.0 8.1 %copy-start = (bf16[32,16384]{1,0:T(8,128)(2,1)S(1)}, bf16[32,16384]{1,0:T(8,128)(2,1)}, u32[]{:S(2)}) copy-start(bf16[32,16384]{1,0:T(8,128)(2,1)} %param.9) | copy-start | bytes 3145732
  0.0 2.9 %copy-start.8 = (s32[64]{0:T(128)S(1)}, s32[64]{0:T(128)}, u32[]{:S(2)}) copy-start(s32[64]{0:T(128)} %param.17) | copy-start | bytes 772
  2.2 5.9 %copy-start.9 = (bf16[64,64]{1,0:T(8,128)(2,1)S(1)}, bf16[64,64]{1,0:T(8,128)(2,1)}, u32[]{:S(2)}) copy-start(bf16[64,64]{1,0:T(8,128)(2,1)} %param.11) | copy-start | bytes 24580
  2.2 5.9 %copy-start.10 = (bf16[32,64]{1,0:T(8,128)(2,1)S(1)}, bf16[32,64]{1,0:T(8,128)(2,1)}, u32[]{:S(2)}) copy-start(bf16[32,64]{1,0:T(8,128)(2,1)} %param.10) | copy-start | bytes 12292
  2.8 1.0 copy-start.2
  2.9 1.0 copy-start.4
  10.7 5.5 %copy-start.6 = (bf16[64,16384]{1,0:T(8,128)(2,1)}, bf16[64,16384]{1,0:T(8,128)(2,1)S(1)}, u32[]{:S(2)}) copy-start(bf16[64,16384]{1,0:T(8,128)(2,1)S(1)} %multiply_convert_fusion.1) | copy-start | bytes 6291460
  10.8 2.9 %copy-start.1 = (bf16[16,8,64,256]{3,0,1,2:T(8,128)(2,1)S(1)}, bf16[16,8,64,256]{3,0,1,2:T(8,128)(2,1)}, u32[]{:S(2)}) copy-start(bf16[16,8,64,256]{3,0,1,2:T(8,128)(2,1)} %multiply_convert_fusion) | copy-start | bytes 12582916
  16.3 4.2 %copy-start.11 = (s32[64]{0:T(128)S(1)}, s32[64]{0:T(128)}, u32[]{:S(2)}) copy-start(s32[64]{0:T(128)} %param.16) | copy-start | bytes 772
  16.3 4.2 %copy-start.12 = (s32[64]{0:T(128)S(1)}, s32[64]{0:T(128)}, u32[]{:S(2)}) copy-start(s32[64]{0:T(128)} %param.15) | copy-start | bytes 772
  132.7 2.3 %copy-start.3 = (f32[16,64,256]{2,0,1:T(8,128)S(1)}, f32[16,64,256]{2,0,1:T(8,128)}, u32[]{:S(2)}) copy-start(f32[16,64,256]{2,0,1:T(8,128)} %copy-done.2) | copy-start | bytes 3145732
  132.7 2.3 %copy-start.5 = (f32[8,64,256]{2,0,1:T(8,128)S(1)}, f32[8,64,256]{2,0,1:T(8,128)}, u32[]{:S(2)}) copy-start(f32[8,64,256]{2,0,1:T(8,128)} %copy-done.4) | copy-start | bytes 1572868
  132.7 2.3 %copy-start.7 = (bf16[64,16384]{1,0:T(8,128)(2,1)S(1)}, bf16[64,16384]{1,0:T(8,128)(2,1)}, u32[]{:S(2)}) copy-start(bf16[64,16384]{1,0:T(8,128)(2,1)} %copy-done.6) | copy-start | bytes 6291460

commit v2 on v1

--- a/solution.py
+++ b/solution.py
@@ -15,7 +15,7 @@
 PAIR = 2
 Z = GZ // PAIR
 MESH = pl.DeviceIdType.MESH
-DIRECTIONS = ((0, 1), (0, -1), (1, 0), (-1, 0), (1, 1), (1, -1), (-1, 1), (-1, -1))
+LEVELS = ((1, 2), (0, 3))
 ORDER = (3, 0, 1, 2)
 OUT_ORDER = (0, 3, 1, 2)
 
@@ -65,29 +65,33 @@
     )
 
 
-def build_band(w_ref, band_ref):
+def build_band(w_ref, band_ref, side_ref):
     channels = w_ref.shape[1]
     width = PAIR * channels
 
     def one(n, carry):
         layer, a = lax.div(n, 3), lax.rem(n, 3)
         band_ref[layer, :, a] = jnp.zeros(band_ref.shape[1:2] + band_ref.shape[3:], band_ref.dtype)
-        for zl in range(2 + PAIR):
-            part, slot = (0, zl - 1) if 1 <= zl <= PAIR else (1, 0 if zl == 0 else 1)
-            for zz in range(PAIR):
-                e = zl - zz
-                if not 0 <= e <= 2:
-                    continue
-                for source, row in ((0, 0), (1, 1), (2, 2), (-1, 3)):
-                    for target in range(PAIR):
-                        b = source - target + 1
-                        if not 0 <= b <= 2:
-                            continue
-                        rows = slice(row * channels, (row + 1) * channels)
-                        lanes = zz * width + target * channels
-                        band_ref[layer, part, a, slot, rows, lanes : lanes + channels] = w_ref[
-                            n * 9 + b * 3 + e
-                        ]
+        side_ref[layer, :, a] = jnp.zeros(side_ref.shape[1:2] + side_ref.shape[3:], side_ref.dtype)
+        for part, levels in enumerate(LEVELS):
+            for slot, zl in enumerate(levels):
+                for zz in range(PAIR):
+                    e = zl - zz
+                    if not 0 <= e <= 2:
+                        continue
+                    for source, row in ((0, 0), (1, 1), (2, 2), (-1, 3)):
+                        for target in range(PAIR):
+                            b = source - target + 1
+                            if not 0 <= b <= 2:
+                                continue
+                            rows = slice(row * channels, (row + 1) * channels)
+                            lanes = zz * width + target * channels
+                            lanes = slice(lanes, lanes + channels)
+                            block = w_ref[n * 9 + b * 3 + e]
+                            band_ref[layer, part, a, slot, rows, lanes] = block
+                            if source in (-1, 2):
+                                rows = slice(slot * channels, (slot + 1) * channels)
+                                side_ref[layer, max(source, 0) // 2, a, part, rows, lanes] = block
         return carry
 
     lax.fori_loop(0, band_ref.shape[0] * 3, one, 0)
@@ -102,7 +106,10 @@
     ids,
     arrived,
     field,
+    edge_out,
+    edge_in,
     band_ref,
+    side_ref,
     totals,
     sum_picks,
     out_picks,
@@ -116,6 +123,8 @@
     x_recv,
     halo_send,
     halo_recv,
+    edge_send,
+    edge_recv,
     rx_send,
     rx_recv,
     rz_send,
@@ -131,12 +140,20 @@
     me_z, me_x = lax.div(me_row, strips), lax.rem(me_row, strips)
     inner = pl.ds(span, blocks)
 
-    def place(dz, ds):
-        strip = me_column * strips + me_x + ds
-        z = me_z + dz
-        present = (strip >= 0) & (strip < columns * strips) & (z >= 0) & (z < Z)
+    def snake(column, x):
+        return x + lax.rem(column, 2) * (strips - 1 - 2 * x)
+
+    me_strip = snake(me_column, me_x)
+
+    def beside(ds):
+        strip = me_column * strips + me_strip + ds
+        present = (strip >= 0) & (strip < columns * strips)
         column = lax.div(strip + strips, strips) - 1
-        return present, column, z * strips + lax.rem(strip + strips, strips)
+        x = snake(column + 2, lax.rem(strip + strips, strips))
+        return present, column, me_z * strips + x
+
+    def above(dz):
+        return (me_z + dz >= 0) & (me_z + dz < Z)
 
     def tell(t):
         return pltpu.make_async_remote_copy(
@@ -171,31 +188,31 @@
         )
 
     def halo(layer, i, k):
-        dz, ds = DIRECTIONS[k]
-        _, column, row = place(dz, ds)
-        pairs = slice(0, PAIR) if ds == 0 else slice(1, 2) if ds > 0 else slice(0, 1)
-        source_z = slice(1, 3) if dz == 0 else slice(2, 3) if dz > 0 else slice(1, 2)
-        target_z = slice(1, 3) if dz == 0 else slice(0, 1) if dz > 0 else slice(3, 4)
-        if ds == 0:
-            source_rows = target_rows = slice(span, span + blocks)
-        elif ds > 0:
-            source_rows, target_rows = slice(blocks, blocks + span), slice(0, span)
-        else:
-            source_rows = slice(span, 2 * span)
-            target_rows = slice(span + blocks, 2 * span + blocks)
+        dz = (1, -1)[k]
         return pltpu.make_async_remote_copy(
-            src_ref=field.at[layer, i + 1, pairs, source_z, source_rows],
-            dst_ref=field.at[layer, i + 1, pairs, target_z, target_rows],
+            src_ref=field.at[layer, i + 1, :, 2 - k, inner],
+            dst_ref=field.at[layer, i + 1, :, 3 * k, inner],
             send_sem=halo_send.at[layer, i, k],
             recv_sem=halo_recv.at[layer, i, k],
+            device_id=(me_column, (me_z + dz) * strips + me_x),
+            device_id_type=MESH,
+        )
+
+    def border(layer, i, part, side):
+        _, column, row = beside((1, -1)[side])
+        return pltpu.make_async_remote_copy(
+            src_ref=edge_out.at[layer, i, side, part],
+            dst_ref=edge_in.at[layer, i + 1, side, part],
+            send_sem=edge_send.at[layer, i, part, side],
+            recv_sem=edge_recv.at[layer, i, part, side],
             device_id=(column, row),
             device_id_type=MESH,
         )
 
     def back_x(i, u):
         return pltpu.make_async_remote_copy(
-            src_ref=dense.at[i, me_x],
-            dst_ref=dense.at[i, me_x],
+            src_ref=dense.at[i, me_strip],
+            dst_ref=dense.at[i, me_strip],
             send_sem=rx_send.at[i, u],
             recv_sem=rx_recv.at[i, u],
             device_id=(me_column, me_z * strips + lax.rem(me_x + u, strips)),
@@ -213,22 +230,30 @@
             device_id_type=MESH,
         )
 
-    def send_halos(layer, i):
-        for k, (dz, ds) in enumerate(DIRECTIONS):
-            present, _, _ = place(dz, ds)
-
-            @pl.when(present)
+    low_half = lax.broadcasted_iota(jnp.int32, (blocks, LANES), 1) < LANES // PAIR
+
+    def send_border(layer, i, part):
+        first, second = LEVELS[part]
+        for side in range(2):
+            rows = slice(blocks, blocks + span) if side == 0 else slice(span, 2 * span)
+            view = field.at[layer, i + 1, 1 - side]
+            tiles = [view[first, rows], view[second, rows]]
+            tiles[side] = pltpu.roll(tiles[side].astype(jnp.float32), LANES // PAIR, 1).astype(
+                jnp.bfloat16
+            )
+            edge_out[layer, i, side, part] = jnp.where(low_half[:span], tiles[0], tiles[1])
+
+            @pl.when(beside((1, -1)[side])[0])
             def _():
-                halo(layer, i, k).start()
-
-    def wait_halos(layer, i, ks):
-        for k in ks:
-            dz, ds = DIRECTIONS[k]
-            present, _, _ = place(-dz, -ds)
-
-            @pl.when(present)
+                border(layer, i, part, side).start()
+
+    def wait_border(layer, i):
+        for side in range(2):
+
+            @pl.when(beside((-1, 1)[side])[0])
             def _():
-                halo(layer, i, k).wait_recv()
+                for part in range(2):
+                    border(layer, i, part, side).wait_recv()
 
     barrier = pltpu.get_barrier_semaphore()
     for t in range(1, rows):
@@ -239,15 +264,14 @@
             device_id_type=MESH,
         )
     expected = rows - 1
-    for dz in (-1, 0, 1):
-        for ds in (-1, 1):
-            present, column, row = place(dz, ds)
-            other = present & (column != me_column)
-            expected = expected + other.astype(jnp.int32)
-
-            @pl.when(other)
-            def _():
-                pl.semaphore_signal(barrier, inc=1, device_id=(column, row), device_id_type=MESH)
+    for ds in (-1, 1):
+        present, column, row = beside(ds)
+        other = present & (column != me_column)
+        expected = expected + other.astype(jnp.int32)
+
+        @pl.when(other)
+        def _():
+            pl.semaphore_signal(barrier, inc=1, device_id=(column, row), device_id_type=MESH)
 
     pl.semaphore_wait(barrier, expected)
 
@@ -261,25 +285,22 @@
     for i in ORDER:
         arrived[i, me_row] = sums_ref[me_z, i]
     ids[me_row] = ids_ref[...]
-    for k, (dz, ds) in enumerate(DIRECTIONS):
-        present, _, _ = place(-dz, -ds)
-
-        @pl.when(jnp.logical_not(present))
+    for k in range(2):
+
+        @pl.when(jnp.logical_not(above((-1, 1)[k])))
         def _():
-            target_z = slice(1, 3) if dz == 0 else slice(0, 1) if dz > 0 else slice(3, 4)
-            pairs = slice(0, PAIR) if ds == 0 else slice(1, 2) if ds > 0 else slice(0, 1)
-            low, high = (
-                (span, span + blocks)
-                if ds == 0
-                else (0, span)
-                if ds > 0
-                else (span + blocks, 2 * span + blocks)
-            )
-            for layer in range(layers):
-                view = field.at[layer, 1 : EDGE + 1, pairs, target_z, low:high]
-                view[...] = jnp.zeros(view.shape, field.dtype)
-
-    build_band(w_ref, band_ref)
+            view = field.at[:, 1 : EDGE + 1, :, 3 * k, inner]
+            view[...] = jnp.zeros(view.shape, field.dtype)
+
+        @pl.when(jnp.logical_not(beside((-1, 1)[k])[0]))
+        def _():
+            view = edge_in.at[:, 1 : EDGE + 1, k]
+            view[...] = jnp.zeros(view.shape, edge_in.dtype)
+
+    for jp, rows_out in ((0, slice(span + blocks, 2 * span + blocks)), (1, slice(0, span))):
+        view = field.at[:, :, jp, :, rows_out]
+        view[...] = jnp.zeros(view.shape, field.dtype)
+    build_band(w_ref, band_ref, side_ref)
     for t in range(1, rows):
         tell(t).wait_recv()
 
@@ -291,7 +312,7 @@
         return jnp.concatenate(parts, axis=1)
 
     for r in range(rows):
-        one_hot = picks(ids[r], me_x * blocks, blocks)
+        one_hot = picks(ids[r], me_strip * blocks, blocks)
         sum_picks[:, r * slots : (r + 1) * slots] = one_hot.T.astype(jnp.bfloat16)
     for z in range(Z):
         out_picks[z * slots : (z + 1) * slots] = picks(
@@ -308,7 +329,13 @@
         for jp in range(PAIR):
             for zz in range(PAIR):
                 field[layer, i + 1, jp, 1 + zz, inner] = tiles(jp, zz)
-        send_halos(layer, i)
+        for k in range(2):
+
+            @pl.when(above((1, -1)[k]))
+            def _():
+                halo(layer, i, k).start()
+
+        send_border(layer, i, 0)
 
     def gather(i):
         for t in range(Z):
@@ -326,31 +353,28 @@
 
         spread(0, i, tiles)
 
-    for n, i in enumerate(ORDER):
-        forward(i)
-        if n > 0:
-            gather(ORDER[n - 1])
-    gather(ORDER[-1])
-
-    low_half = lax.broadcasted_iota(jnp.int32, (blocks, LANES), 1) < LANES // PAIR
-
-    def shift(layer, down, levels):
-        source, target = (EDGE, 0) if down else (1, EDGE + 1)
-        for jp in range(PAIR):
-            low = 0 if jp == 1 else span
-            size = blocks + span
-            ranks = lax.broadcasted_iota(jnp.int32, (size, LANES), 0)
-            edge_rank = 0 if down else span - 1
-            keep = lax.rem(ranks, span) != edge_rank
-            for zl in levels:
-                moved = pltpu.roll(
-                    field[layer, source, jp, zl, low : low + size].astype(jnp.float32),
-                    1 if down else size - 1,
-                    0,
-                )
-                field[layer, target, jp, zl, low : low + size] = jnp.where(
-                    keep, moved, 0.0
-                ).astype(jnp.bfloat16)
+    def shifted(tile, down):
+        size = tile.shape[0]
+        ranks = lax.broadcasted_iota(jnp.int32, tile.shape, 0)
+        keep = lax.rem(ranks, span) != (0 if down else span - 1)
+        moved = pltpu.roll(tile.astype(jnp.float32), 1 if down else size - 1, 0)
+        return jnp.where(keep, moved, 0.0).astype(jnp.bfloat16)
+
+    def shift(layer, i, levels):
+        for down, phase, target in ((True, EDGE - 1, 0), (False, 0, EDGE + 1)):
+            if phase == i:
+                for jp in range(PAIR):
+                    for zl in levels:
+                        view = field.at[layer, :, jp, zl]
+                        view[target, inner] = shifted(view[i + 1, inner], down)
+
+    def shift_edges(layer, i):
+        for down, phase, target in ((True, EDGE - 1, 0), (False, 0, EDGE + 1)):
+            if phase == i:
+                for side in range(2):
+                    for part in range(2):
+                        view = edge_in.at[layer, :, side, part]
+                        view[target] = shifted(view[i + 1], down)
 
     def windows(layer, i, jp, levels):
         parts = []
@@ -366,49 +390,94 @@
         return jnp.concatenate(parts, axis=1)
 
     def conv_terms(layer, i, part):
-        levels = (1, 2) if part == 0 else (0, 3)
         weight = band_ref[layer, part].reshape(-1, band_ref.shape[5])
-        lhs = jnp.concatenate([windows(layer, i, jp, levels) for jp in range(PAIR)], axis=0)
+        lhs = jnp.concatenate(
+            [windows(layer, i, jp, LEVELS[part]) for jp in range(PAIR)], axis=0
+        )
         return jnp.dot(lhs, weight, preferred_element_type=jnp.float32)
 
-    beside = [k for k, (dz, _) in enumerate(DIRECTIONS) if dz == 0]
-    across = [k for k, (dz, _) in enumerate(DIRECTIONS) if dz != 0]
+    def own_terms(layer, i):
+        totals[i] = conv_terms(layer, i, 0)
+
+    def edge_terms(layer, i):
+        for side in range(2):
+            lhs = jnp.concatenate(
+                [edge_in[layer, i + a, side, part] for a in range(3) for part in range(2)], axis=1
+            )
+            weight = side_ref[layer, side].reshape(-1, side_ref.shape[5])
+            rows_in = slice(0, span) if side == 0 else slice(2 * blocks - span, 2 * blocks)
+            totals[i, rows_in] += jnp.dot(lhs, weight, preferred_element_type=jnp.float32)
+
+    def finish(layer, i):
+        total = totals[i]
+        activated = (total / (1.0 + jnp.exp(-total))).astype(jnp.bfloat16)
+
+        def tiles(jp, zz):
+            return activated[jp * blocks : (jp + 1) * blocks, zz * LANES : (zz + 1) * LANES]
+
+        if layer < layers - 1:
+            spread(layer + 1, i, tiles)
+            shift(layer + 1, i, LEVELS[0])
+        else:
+            for jp in range(PAIR):
+                for zz in range(PAIR):
+                    low = (jp * PAIR + zz) * LANES
+                    dense[i, me_strip, :, low : low + LANES] = tiles(jp, zz)
+            for u in range(1, strips):
+                back_x(i, u).start()
+
+    def ready(i, done):
+        return {(i - 1) % EDGE, i, (i + 1) % EDGE} <= set(done)
+
+    for n, i in enumerate(ORDER):
+        forward(i)
+        if n > 0:
+            gather(ORDER[n - 1])
+            shift(0, ORDER[n - 1], LEVELS[0])
+    for i in OUT_ORDER:
+        if ready(i, ORDER[:-1]):
+            own_terms(0, i)
+    gather(ORDER[-1])
+    shift(0, ORDER[-1], LEVELS[0])
+    for i in OUT_ORDER:
+        if not ready(i, ORDER[:-1]):
+            own_terms(0, i)
+
     for layer in range(layers):
         before = ORDER if layer == 0 else OUT_ORDER
-        for i in before:
-            wait_halos(layer, i, beside)
-        shift(layer, True, (1, 2))
-        shift(layer, False, (1, 2))
-        for i in OUT_ORDER:
-            totals[i] = conv_terms(layer, i, 0)
-        waited = set()
-        for i in OUT_ORDER:
-            needed = {(i - 1) % EDGE, i, (i + 1) % EDGE}
+        if layer > 0:
+            for i in OUT_ORDER:
+                own_terms(layer, i)
+        reached, bordered = [], []
+
+        def reach(i):
             for phase in before:
-                if phase in needed and phase not in waited:
-                    wait_halos(layer, phase, across)
-                    waited.add(phase)
-                    if phase == EDGE - 1:
-                        shift(layer, True, (0, 3))
-                    if phase == 0:
-                        shift(layer, False, (0, 3))
-            total = totals[i] + conv_terms(layer, i, 1)
-            activated = (total / (1.0 + jnp.exp(-total))).astype(jnp.bfloat16)
-
-            def tiles(jp, zz):
-                return activated[
-                    jp * blocks : (jp + 1) * blocks, zz * LANES : (zz + 1) * LANES
-                ]
-
-            if layer < layers - 1:
-                spread(layer + 1, i, tiles)
-            else:
-                for jp in range(PAIR):
-                    for zz in range(PAIR):
-                        low = (jp * PAIR + zz) * LANES
-                        dense[i, me_x, :, low : low + LANES] = tiles(jp, zz)
-                for u in range(1, strips):
-                    back_x(i, u).start()
+                if phase in {(i - 1) % EDGE, i, (i + 1) % EDGE} and phase not in reached:
+                    for k in range(2):
+
+                        @pl.when(above((-1, 1)[k]))
+                        def _():
+                            halo(layer, phase, k).wait_recv()
+
+                    send_border(layer, phase, 1)
+                    shift(layer, phase, LEVELS[1])
+                    reached.append(phase)
+
+        def close(i):
+            for phase in before:
+                if phase in {(i - 1) % EDGE, i, (i + 1) % EDGE} and phase not in bordered:
+                    wait_border(layer, phase)
+                    shift_edges(layer, phase)
+                    bordered.append(phase)
+            edge_terms(layer, i)
+            finish(layer, i)
+
+        for n, i in enumerate(OUT_ORDER):
+            reach(i)
+            totals[i] += conv_terms(layer, i, 1)
+            if n > 0:
+                close(OUT_ORDER[n - 1])
+        close(OUT_ORDER[-1])
 
     for i in OUT_ORDER:
         for u in range(1, strips):
@@ -435,12 +504,16 @@
             for t in range(Z):
                 along_x(i, t, u).wait_send()
         for layer in range(layers):
-            for k, (dz, ds) in enumerate(DIRECTIONS):
-                present, _, _ = place(dz, ds)
-
-                @pl.when(present)
+            for k in range(2):
+
+                @pl.when(above((1, -1)[k]))
                 def _():
                     halo(layer, i, k).wait_send()
+
+                @pl.when(beside((1, -1)[k])[0])
+                def _():
+                    for part in range(2):
+                        border(layer, i, part, k).wait_send()
 
 
 def exchange_and_convolve(ids, sums, w_conv):
@@ -450,7 +523,8 @@
     layers, channels = w_conv.shape[0], w_conv.shape[4]
     span = rows * (TX // EDGE)
     blocks = span * (TY // EDGE) // strips
-    halos = (layers, EDGE, len(DIRECTIONS))
+    halos = (layers, EDGE, 2)
+    borders = halos + (2,)
     dma = pltpu.SemaphoreType.DMA
     return pl.pallas_call(
         functools.partial(conv_kernel, (rows, columns)),
@@ -461,7 +535,10 @@
             pltpu.VMEM((rows, slots, LANES), jnp.int32),
             pltpu.VMEM((EDGE, rows, slots, width), jnp.bfloat16),
             pltpu.VMEM((layers, EDGE + 2, PAIR, PAIR + 2, blocks + 2 * span, LANES), jnp.bfloat16),
+            pltpu.VMEM(borders + (span, LANES), jnp.bfloat16),
+            pltpu.VMEM((layers, EDGE + 2, 2, 2, span, LANES), jnp.bfloat16),
             pltpu.VMEM((layers, 2, 3, 2, 2 * LANES, 2 * LANES), jnp.bfloat16),
+            pltpu.VMEM((layers, 2, 3, 2, LANES, 2 * LANES), jnp.bfloat16),
             pltpu.VMEM((EDGE, PAIR * blocks, 2 * LANES), jnp.float32),
             pltpu.VMEM((blocks, rows * slots), jnp.bfloat16),
             pltpu.VMEM((Z * slots, strips * blocks), jnp.bfloat16),
@@ -475,6 +552,8 @@
             dma((EDGE, Z, strips)),
             dma(halos),
             dma(halos),
+            dma(borders),
+            dma(borders),
             dma((EDGE, strips)),
             dma((EDGE, strips)),
             dma((EDGE, Z)),

time: 139 us -> 131 us (0.942)
  Pallas kernels: 107 us -> 99.5 us
    pallas_call x1, Pallas kernels: 107 us -> 99.5 us  [exchange_and_convolve(): pl.pallas_call(functools.partial(conv_kernel, (rows, columns)), out_shape...]
where the time goes in v2:
time: 131 us
  Pallas kernels  99.5 us (76%)
  local copies, waits for them, and re-layouts  19.3 us (15%)
  matrix products  6.67 us (5%)
  other arithmetic  4.94 us (4%)
    pallas_call x1, Pallas kernels, exchange_and_convolve(): pl.pallas_call(functools.partial(conv_kernel, (rows, columns)), out_shape...  99.5 us
    unnamed x29, local copies, waits for them, and re-layouts  6.01 us
    reshape x1, local copies, waits for them, and re-layouts, interpolate(): cells = blocks.reshape(Z, EDGE, slots, EDGE // PAIR, PAIR, PAIR, channels)  4.65 us
    convert_element_type x1, other arithmetic, trilinear(): return corner_weights.astype(jnp.bfloat16)  4.09 us
    dot_general x1, matrix products, point_layer(): lax.dot_general(weight, inputs, (((0,), (0,)), ((), ())), preferred_eleme...  2.68 us

profile of v2, /device:TPU:0, one launch (start us, length us, event | category | flops | bytes accessed | tf_op | source)
XLA Modules:
  0.0 130.6 jit_solution(4064950168066569526)
XLA Ops:
  0.0 1.1 copy.43
  1.1 1.0 copy.44
  2.2 0.0 copy-start.9
  2.2 0.0 copy-start.10
  2.2 0.6 add_multiply_fusion
  2.8 0.1 select_add_fusion
  3.0 0.1 fusion.10
  3.0 0.7 copy-done.2
  3.7 0.2 copy-done.4
  4.0 4.1 %multiply_convert_fusion = bf16[16,8,64,256]{3,0,1,2:T(8,128)(2,1)} fusion(f32[64,256]{1,0:T(8,128)S(1)} %fusion.10, f32[8,64,256]{2,0,1:T(8,128)S(1)} %select_add_fusion, f32[16,64,256]{2,0,1:T(8,128)S(1)} %add_multiply_fusion), kind=kLoop, calls=%fused_computation.1 | loop fusion | flops 6291456 | bytes 5832704 | tf_op jit(solution)/shard_map/convert_element_type | solution.py:47
  8.1 2.7 %multiply_convert_fusion.1 = bf16[64,16384]{1,0:T(8,128)(2,1)S(1)} fusion(bf16[64,64]{1,0:T(8,128)(2,1)S(1)} %copy-done.9, bf16[32,64]{1,0:T(8,128)(2,1)S(1)} %copy-done.10, bf16[32,16384]{1,0:T(8,128)(2,1)S(1)} %copy-done), kind=kOutput, calls=%fused_computation.7 | convolution fusion | flops 211812352 | bytes 3158016 | tf_op jit(solution)/shard_map/dot_general | solution.py:24
  10.7 0.0 copy-start.6
  10.8 0.5 copy.29
  11.3 2.4 %copy-done.1 = bf16[16,8,64,256]{3,0,1,2:T(8,128)(2,1)S(1)} copy-done((bf16[16,8,64,256]{3,0,1,2:T(8,128)(2,1)S(1)}, bf16[16,8,64,256]{3,0,1,2:T(8,128)(2,1)}, u32[]{:S(2)}) %copy-start.1) | copy-done | bytes 4194328
  13.7 2.6 %fusion.5 = bf16[64,16,8,64]{3,2,1,0:T(8,128)(2,1)S(1)} fusion(bf16[64,64,256,1]{2,1,0,3:T(8,128)(2,1)S(1)} %bitcast.76, bf16[16,8,64,256]{3,0,1,2:T(8,128)(2,1)S(1)} %copy-done.1), kind=kOutput, calls=%fused_computation.12 | convolution fusion | flops 268959744 | bytes 7340032 | tf_op jit(solution)/shard_map/czsp,hsp->sczh/dot_general | solution.py:51
  16.3 0.0 copy-start.11
  16.3 2.2 %copy.42 = bf16[64,4,2,2,4,2,64]{6,3,5,2,0,1,4:T(2,128)(2,1)S(1)} copy(bf16[64,4,2,2,4,2,64]{6,5,4,3,2,1,0:T(2,128)(2,1)S(1)} %bitcast.75) | data formatting | bytes 2097152 | tf_op jit(solution)/shard_map/reshape | solution.py:54
  18.5 2.1 %reshape.93.sums_ref = bf16[4,4,64,512]{3,2,1,0:T(8,128)(2,1)} reshape(bf16[4,4,64,2,2,2,64]{6,5,4,3,2,1,0:T(2,128)(2,1)S(1)} %bitcast.70) | data formatting | bytes 2097152 | tf_op jit(solution)/shard_map/reshape | solution.py:56
  20.6 0.7 broadcast_in_dim.74.ids_ref
  21.2 99.5 %shard_map.91 = bf16[4,4,64,512]{3,2,1,0:T(8,128)(2,1)} custom-call(s32[64,128]{1,0:T(8,128)} %broadcast_in_dim.74.ids_ref, bf16[4,4,64,512]{3,2,1,0:T(8,128)(2,1)} %reshape.93.sums_ref, bf16[54,64,64]{2,1,0:T(8,128)(2,1)} %bitcast.77), custom_call_target="tpu_custom_call" | custom-call | tf_op jit(solution)/shard_map/pallas_call | solution.py:529
  120.7 4.7 %reshape.95 = bf16[4,4,64,2,2,2,64]{6,5,4,3,2,1,0:T(2,128)(2,1)S(1)} reshape(bf16[4,4,64,512]{3,2,1,0:T(8,128)(2,1)} %shard_map.91) | data formatting | bytes 2097152 | tf_op jit(solution)/shard_map/reshape | solution.py:61
  125.4 2.3 %copy.19 = bf16[64,4,2,2,4,2,64]{6,3,2,1,5,4,0:T(2,128)(2,1)S(1)} copy(bf16[64,4,2,2,4,2,64]{6,3,5,2,0,1,4:T(2,128)(2,1)S(1)} %bitcast.71) | data formatting | bytes 2097152 | tf_op jit(solution)/shard_map/transpose | solution.py:62
  127.7 1.4 %fusion.3 = bf16[64,8,8,256]{3,2,1,0:T(8,128)(2,1)S(1)} fusion(bf16[8,64,8,256]{3,2,1,0:T(8,128)(2,1)S(1)} %bitcast.73, bf16[64,16,8,64]{3,1,2,0:T(8,128)(2,1)S(1)} %bitcast.74, f32[64,256]{1,0:T(8,128)S(1)} %fusion.10, f32[8,64,256]{2,0,1:T(8,128)S(1)} %copy-done.5, f32[16,64,256]{2,0,1:T(8,128)S(1)} %copy-done.3), kind=kOutput, calls=%fused_computation.9 | convolution fusion | flops 279969792 | bytes 6881280 | tf_op jit(solution)/shard_map/czsp,sczh->hsp/dot_general | solution.py:63
  129.2 1.5 %copy.26 = bf16[64,8,8,256]{3,2,0,1:T(8,128)(2,1)} copy(bf16[64,8,8,256]{3,2,1,0:T(8,128)(2,1)S(1)} %fusion.3) | data formatting | bytes 4194304 | tf_op jit(solution)/shard_map/reshape | solution.py:591
  (23 shorter events, 0.1 us)
Async XLA Ops:
  0.0 8.1 %copy-start = (bf16[32,16384]{1,0:T(8,128)(2,1)S(1)}, bf16[32,16384]{1,0:T(8,128)(2,1)}, u32[]{:S(2)}) copy-start(bf16[32,16384]{1,0:T(8,128)(2,1)} %param.9) | copy-start | bytes 3145732
  0.0 2.9 %copy-start.8 = (s32[64]{0:T(128)S(1)}, s32[64]{0:T(128)}, u32[]{:S(2)}) copy-start(s32[64]{0:T(128)} %param.17) | copy-start | bytes 772
  2.2 5.9 %copy-start.9 = (bf16[64,64]{1,0:T(8,128)(2,1)S(1)}, bf16[64,64]{1,0:T(8,128)(2,1)}, u32[]{:S(2)}) copy-start(bf16[64,64]{1,0:T(8,128)(2,1)} %param.11) | copy-start | bytes 24580
  2.2 5.9 %copy-start.10 = (bf16[32,64]{1,0:T(8,128)(2,1)S(1)}, bf16[32,64]{1,0:T(8,128)(2,1)}, u32[]{:S(2)}) copy-start(bf16[32,64]{1,0:T(8,128)(2,1)} %param.10) | copy-start | bytes 12292
  2.8 1.0 copy-start.2
  2.9 1.0 copy-start.4
  10.7 5.5 %copy-start.6 = (bf16[64,16384]{1,0:T(8,128)(2,1)}, bf16[64,16384]{1,0:T(8,128)(2,1)S(1)}, u32[]{:S(2)}) copy-start(bf16[64,16384]{1,0:T(8,128)(2,1)S(1)} %multiply_convert_fusion.1) | copy-start | bytes 6291460
  10.8 2.9 %copy-start.1 = (bf16[16,8,64,256]{3,0,1,2:T(8,128)(2,1)S(1)}, bf16[16,8,64,256]{3,0,1,2:T(8,128)(2,1)}, u32[]{:S(2)}) copy-start(bf16[16,8,64,256]{3,0,1,2:T(8,128)(2,1)} %multiply_convert_fusion) | copy-start | bytes 12582916
  16.3 4.2 %copy-start.11 = (s32[64]{0:T(128)S(1)}, s32[64]{0:T(128)}, u32[]{:S(2)}) copy-start(s32[64]{0:T(128)} %param.16) | copy-start | bytes 772
  16.3 4.2 %copy-start.12 = (s32[64]{0:T(128)S(1)}, s32[64]{0:T(128)}, u32[]{:S(2)}) copy-start(s32[64]{0:T(128)} %param.15) | copy-start | bytes 772
  125.4 2.3 %copy-start.3 = (f32[16,64,256]{2,0,1:T(8,128)S(1)}, f32[16,64,256]{2,0,1:T(8,128)}, u32[]{:S(2)}) copy-start(f32[16,64,256]{2,0,1:T(8,128)} %copy-done.2) | copy-start | bytes 3145732
  125.4 2.3 %copy-start.5 = (f32[8,64,256]{2,0,1:T(8,128)S(1)}, f32[8,64,256]{2,0,1:T(8,128)}, u32[]{:S(2)}) copy-start(f32[8,64,256]{2,0,1:T(8,128)} %copy-done.4) | copy-start | bytes 1572868
  125.4 2.3 %copy-start.7 = (bf16[64,16384]{1,0:T(8,128)(2,1)S(1)}, bf16[64,16384]{1,0:T(8,128)(2,1)}, u32[]{:S(2)}) copy-start(bf16[64,16384]{1,0:T(8,128)(2,1)} %copy-done.6) | copy-start | bytes 6291460

commit v3 on v2

--- a/solution.py
+++ b/solution.py
@@ -14,55 +14,183 @@
 LANES = 128
 PAIR = 2
 Z = GZ // PAIR
+GROUP = 16
 MESH = pl.DeviceIdType.MESH
 LEVELS = ((1, 2), (0, 3))
 ORDER = (3, 0, 1, 2)
 OUT_ORDER = (0, 3, 1, 2)
 
 
+def silu(total):
+    return (total / (1.0 + jnp.exp(-total))).astype(jnp.bfloat16)
+
+
 def point_layer(weight, inputs):
-    mixed_sum = lax.dot_general(
-        weight, inputs, (((0,), (0,)), ((), ())), preferred_element_type=jnp.float32
+    return silu(
+        lax.dot_general(
+            weight, inputs, (((0,), (0,)), ((), ())), preferred_element_type=jnp.float32
+        )
     )
-    return jax.nn.silu(mixed_sum).astype(jnp.bfloat16)
-
-
-def axis_weights(offset, corner, positions):
-    positions = positions[:, None, None]
-    below_part = jnp.where(positions == corner[None], 1.0 - offset[None], 0.0)
-    above_part = jnp.where(positions == corner[None] + 1, offset[None], 0.0)
-    return below_part + above_part
-
-
-def trilinear(offsets, corners, counts, block_edge, grid_depth):
-    slot_width = offsets.shape[2]
-    live_mask = (jnp.arange(slot_width, dtype=jnp.int32)[None, :] < counts[:, None]).astype(
-        jnp.float32
+
+
+def slot_weights(offsets, corners, count):
+    width = offsets.shape[1]
+    ranks = lax.broadcasted_iota(jnp.int32, (GZ, width), 0)
+    live = lax.broadcasted_iota(jnp.int32, (GZ, width), 1) < count
+
+    def axis(position, offset, corner):
+        below_part = jnp.where(position == corner, 1.0 - offset, 0.0)
+        above_part = jnp.where(position == corner + 1, offset, 0.0)
+        return below_part + above_part
+
+    first = ranks < EDGE
+    along_xy = axis(
+        lax.rem(ranks, EDGE),
+        jnp.where(first, offsets[0:1], offsets[1:2]),
+        jnp.where(first, corners[0:1], corners[1:2]),
     )
-    cells = jnp.arange(block_edge * block_edge, dtype=jnp.int32)
-    along_x = axis_weights(offsets[0], corners[0], cells // block_edge)
-    along_y = axis_weights(offsets[1], corners[1], cells % block_edge)
-    along_z = axis_weights(offsets[2], corners[2], jnp.arange(grid_depth, dtype=jnp.int32))
-    corner_weights = (along_x * along_y)[:, None] * along_z[None] * live_mask
-    return corner_weights.astype(jnp.bfloat16)
-
-
-def splat(weights, hidden):
-    sums = jnp.einsum("czsp,hsp->sczh", weights, hidden, preferred_element_type=jnp.float32)
-    slots, channels = sums.shape[0], sums.shape[3]
-    sums = sums.astype(jnp.bfloat16)
-    sums = sums.reshape(slots, EDGE, EDGE // PAIR, PAIR, Z, PAIR, channels)
-    sums = sums.transpose(4, 1, 0, 2, 5, 3, 6)
-    return sums.reshape(Z, EDGE, slots, EDGE * PAIR * channels)
-
-
-def interpolate(weights, blocks):
-    slots, channels = blocks.shape[2], blocks.shape[3] // (EDGE * PAIR)
-    cells = blocks.reshape(Z, EDGE, slots, EDGE // PAIR, PAIR, PAIR, channels)
-    cells = cells.transpose(2, 1, 3, 5, 0, 4, 6).reshape(slots, EDGE * EDGE, GZ, channels)
-    return jnp.einsum("czsp,sczh->hsp", weights, cells, preferred_element_type=jnp.float32).astype(
-        jnp.bfloat16
-    )
+    along_z = jnp.where(live, axis(ranks, offsets[2:3], corners[2:3]), 0.0)
+    rows = []
+    for parity in range(PAIR):
+        for i in range(EDGE):
+            for jp in range(EDGE // PAIR):
+                j = EDGE + jp * PAIR + parity
+                rows.append(along_xy[i : i + 1] * along_xy[j : j + 1] * along_z)
+    return jnp.concatenate(rows, axis=0).astype(jnp.bfloat16)
+
+
+def splat_kernel(
+    span,
+    dest_ref,
+    block_ref,
+    count_ref,
+    features_ref,
+    w_in_ref,
+    w_mid_ref,
+    frac_ref,
+    base_ref,
+    sums_ref,
+    hidden_ref,
+    ids_ref,
+    swap_ref,
+):
+    group = sums_ref.shape[2]
+    width = hidden_ref.shape[1] // group
+    half = EDGE * EDGE // PAIR * GZ
+    along, across = TX // EDGE, TY // EDGE
+    start = pl.program_id(0) * group
+    hidden_one = point_layer(w_in_ref[...], features_ref[...])
+    hidden_two = point_layer(w_mid_ref[...], hidden_one)
+    hidden_ref[...] = hidden_two
+    for s in range(group):
+        points = slice(s * width, (s + 1) * width)
+        weights = slot_weights(frac_ref[:, points], base_ref[:, points], count_ref[start + s])
+        sums = lax.dot_general(
+            weights,
+            hidden_two[:, points],
+            (((1,), (1,)), ((), ())),
+            preferred_element_type=jnp.float32,
+        )
+        swap_ref[s * half : (s + 1) * half] = jnp.concatenate([sums[:half], sums[half:]], axis=1)
+        dest, block = dest_ref[start + s], block_ref[start + s]
+        number = lax.rem(block, across) * span + dest * along + lax.div(block, across)
+        ids_ref[s : s + 1] = jnp.full((1, ids_ref.shape[1]), number, jnp.int32)
+    for i in range(EDGE):
+        for jp in range(EDGE // PAIR):
+            for z in range(GZ):
+                row = (i * (EDGE // PAIR) + jp) * GZ + z
+                low = (jp * PAIR + z % PAIR) * LANES
+                sums_ref[z // PAIR, i, :, low : low + LANES] = swap_ref[
+                    pl.ds(row, group, stride=half)
+                ].astype(jnp.bfloat16)
+
+
+def interpolate_kernel(count_ref, cells_ref, hidden_ref, frac_ref, base_ref, out_ref, swap_ref):
+    group = cells_ref.shape[2]
+    width = hidden_ref.shape[1] // group
+    channels = hidden_ref.shape[0]
+    half = EDGE * EDGE // PAIR * GZ
+    start = pl.program_id(0) * group
+    for i in range(EDGE):
+        for jp in range(EDGE // PAIR):
+            for z in range(GZ):
+                row = (i * (EDGE // PAIR) + jp) * GZ + z
+                low = (jp * PAIR + z % PAIR) * LANES
+                swap_ref[row * group : (row + 1) * group] = cells_ref[
+                    z // PAIR, i, :, low : low + LANES
+                ].astype(jnp.float32)
+    for s in range(group):
+        points = slice(s * width, (s + 1) * width)
+        weights = slot_weights(frac_ref[:, points], base_ref[:, points], count_ref[start + s])
+        cells = swap_ref[pl.ds(s, half, stride=group)].T
+        cells = jnp.concatenate([cells[:channels], cells[channels:]], axis=1).astype(jnp.bfloat16)
+        interp = jnp.dot(cells, weights, preferred_element_type=jnp.float32).astype(jnp.bfloat16)
+        out_ref[:, points] = (
+            hidden_ref[:, points].astype(jnp.float32) + interp.astype(jnp.float32)
+        ).astype(jnp.bfloat16)
+
+
+def grouped(extent, dimension, groups):
+    block = tuple(n // groups if d == dimension else n for d, n in enumerate(extent))
+    return pl.BlockSpec(block, lambda g: tuple(g if d == dimension else 0 for d in range(len(extent))))
+
+
+def whole(extent):
+    return pl.BlockSpec(extent, lambda g: (0,) * len(extent))
+
+
+def splat(features, w_in, w_mid, frac, base, dest, block, count, span):
+    slots, channels = dest.shape[0], w_mid.shape[1]
+    groups = max(1, slots // GROUP)
+    sums = (Z, EDGE, slots, EDGE * PAIR * channels)
+    hidden = (channels, features.shape[1])
+    half = EDGE * EDGE // PAIR * GZ
+    smem = pl.BlockSpec(memory_space=pltpu.SMEM)
+    return pl.pallas_call(
+        functools.partial(splat_kernel, span),
+        grid=(groups,),
+        out_shape=(
+            jax.ShapeDtypeStruct(sums, jnp.bfloat16),
+            jax.ShapeDtypeStruct(hidden, jnp.bfloat16),
+            jax.ShapeDtypeStruct((slots, LANES), jnp.int32),
+        ),
+        in_specs=[
+            smem,
+            smem,
+            smem,
+            grouped(features.shape, 1, groups),
+            whole(w_in.shape),
+            whole(w_mid.shape),
+            grouped(frac.shape, 1, groups),
+            grouped(base.shape, 1, groups),
+        ],
+        out_specs=(
+            grouped(sums, 2, groups),
+            grouped(hidden, 1, groups),
+            grouped((slots, LANES), 0, groups),
+        ),
+        scratch_shapes=[pltpu.VMEM((slots // groups * half, PAIR * channels), jnp.float32)],
+    )(dest, block, count, features, w_in, w_mid, frac, base)
+
+
+def interpolate(cells, hidden, frac, base, count):
+    slots, channels = count.shape[0], hidden.shape[0]
+    groups = max(1, slots // GROUP)
+    half = EDGE * EDGE // PAIR * GZ
+    return pl.pallas_call(
+        interpolate_kernel,
+        grid=(groups,),
+        out_shape=jax.ShapeDtypeStruct(hidden.shape, jnp.bfloat16),
+        in_specs=[
+            pl.BlockSpec(memory_space=pltpu.SMEM),
+            grouped(cells.shape, 2, groups),
+            grouped(hidden.shape, 1, groups),
+            grouped(frac.shape, 1, groups),
+            grouped(base.shape, 1, groups),
+        ],
+        out_specs=grouped(hidden.shape, 1, groups),
+        scratch_shapes=[pltpu.VMEM((slots // groups * half, PAIR * channels), jnp.float32)],
+    )(count, cells, hidden, frac, base)
 
 
 def build_band(w_ref, band_ref, side_ref):
@@ -410,7 +538,7 @@
 
     def finish(layer, i):
         total = totals[i]
-        activated = (total / (1.0 + jnp.exp(-total))).astype(jnp.bfloat16)
+        activated = silu(total)
 
         def tiles(jp, zz):
             return activated[jp * blocks : (jp + 1) * blocks, zz * LANES : (zz + 1) * LANES]
@@ -566,29 +694,12 @@
 def per_device(
     features, w_in, w_mid, w_conv, point_frac, point_base, slot_dest, slot_tile_block, slot_count
 ):
-    slot_total = slot_dest.shape[0]
-    slot_width = features.shape[1] // slot_total
     span = lax.axis_size("grid") * (TX // EDGE)
-    along, across = TX // EDGE, TY // EDGE
-    hidden_one = point_layer(w_in, features)
-    hidden_two = point_layer(w_mid, hidden_one)
-    channels = hidden_two.shape[0]
-    hidden_two = hidden_two.reshape(channels, slot_total, slot_width)
-    offsets, corners = lax.optimization_barrier(
-        (
-            point_frac.reshape(3, slot_total, slot_width),
-            point_base.reshape(3, slot_total, slot_width),
-        )
+    sums, hidden, ids = splat(
+        features, w_in, w_mid, point_frac, point_base, slot_dest, slot_tile_block, slot_count, span
     )
-    block_x = slot_dest * along + slot_tile_block // across
-    block_y = slot_tile_block % across
-    ids = jnp.broadcast_to((block_y * span + block_x)[:, None], (slot_total, LANES))
-    weights = trilinear(offsets, corners, slot_count, EDGE, GZ)
-    local_sums = splat(weights, hidden_two)
-    blocks = exchange_and_convolve(ids, local_sums, w_conv)
-    interp = interpolate(weights, blocks)
-    point_out = (hidden_two.astype(jnp.float32) + interp.astype(jnp.float32)).astype(jnp.bfloat16)
-    return point_out.reshape(channels, slot_total * slot_width)
+    cells = exchange_and_convolve(ids, sums, w_conv)
+    return interpolate(cells, hidden, point_frac, point_base, slot_count)
 
 
 def solution(mesh):

time: 131 us -> 114 us (0.87)
  local copies, waits for them, and re-layouts: 19.3 us -> 0 us
  Pallas kernels: 99.5 us -> 114 us
  matrix products: 6.67 us -> 0 us
  other arithmetic: 4.94 us -> 0 us
    pallas_call x0 -> x2, Pallas kernels: none -> 14.5 us  [the longest x1 8.64 us: splat(): pl.pallas_call(functools.partial(splat_kernel, span), grid=(groups,), out...]
    reshape x4 -> x0, local copies, waits for them, and re-layouts: 10.3 us -> none  [the longest x1 4.65 us: interpolate(): cells = blocks.reshape(Z, EDGE, slots, EDGE // PAIR, PAIR, PAIR, channels)]
    dot_general x3 -> x0, matrix products: 6.67 us -> none  [the longest x1 2.68 us: point_layer(): lax.dot_general(weight, inputs, (((0,), (0,)), ((), ())), preferred_eleme...]
    unnamed x29 -> x0, local copies, waits for them, and re-layouts: 6.01 us -> none
    convert_element_type x2 -> x0, other arithmetic: 4.16 us -> none  [the longest x1 4.09 us: trilinear(): return corner_weights.astype(jnp.bfloat16)]
    transpose x1 -> x0, local copies, waits for them, and re-layouts: 2.29 us -> none  [interpolate(): cells.transpose(2, 1, 3, 5, 0, 4, 6)]
where the time goes in v3:
time: 114 us
  Pallas kernels  114 us (100%)
    pallas_call x1, Pallas kernels, exchange_and_convolve(): pl.pallas_call(functools.partial(conv_kernel, (rows, columns)), out_shape...  99.5 us
    pallas_call x1, Pallas kernels, splat(): pl.pallas_call(functools.partial(splat_kernel, span), grid=(groups,), out...  8.64 us
    pallas_call x1, Pallas kernels, interpolate(): pl.pallas_call(interpolate_kernel, grid=(groups,), out_shape=jax.ShapeDty...  5.85 us

profile of v3, /device:TPU:0, one launch (start us, length us, event | category | flops | bytes accessed | tf_op | source)
XLA Modules:
  0.0 114.0 jit_solution(5881377093420040661)
XLA Ops:
  0.0 8.6 %shard_map.91 = (bf16[4,4,64,512]{3,2,1,0:T(8,128)(2,1)}, bf16[64,16384]{1,0:T(8,128)(2,1)}, s32[64,128]{1,0:T(8,128)}) custom-call(s32[64]{0:T(128)} %dest_ref.1, s32[64]{0:T(128)} %block_ref.1, s32[64]{0:T(128)} %count_ref.3, bf16[32,16384]{1,0:T(8,128)(2,1)} %features_ref.1, bf16[32,64]{1,0:T(8,128)(2,1)} %w_in_ref.1, bf16[64,64]{1,0:T(8,128)(2,1)} %w_mid_ref.1, ...), custom_call_target="tpu_custom_call" | custom-call | tf_op jit(solution)/shard_map/pallas_call | solution.py:149
  8.6 99.5 %shard_map.92.cells_ref = bf16[4,4,64,512]{3,2,1,0:T(8,128)(2,1)} custom-call(s32[64,128]{1,0:T(8,128)} %get-tuple-element.8.ids_ref, bf16[4,4,64,512]{3,2,1,0:T(8,128)(2,1)} %get-tuple-element.9.sums_ref, bf16[54,64,64]{2,1,0:T(8,128)(2,1)} %bitcast.1), custom_call_target="tpu_custom_call" | custom-call | tf_op jit(solution)/shard_map/pallas_call | solution.py:657
  108.1 5.8 %shard_map.93 = bf16[64,16384]{1,0:T(8,128)(2,1)} custom-call(s32[64]{0:T(128)} %count_ref.3, bf16[4,4,64,512]{3,2,1,0:T(8,128)(2,1)} %shard_map.92.cells_ref, bf16[64,16384]{1,0:T(8,128)(2,1)} %get-tuple-element.10.hidden_ref, f32[3,16384]{1,0:T(4,128)} %frac_ref.3, s32[3,16384]{1,0:T(4,128)} %base_ref.3), custom_call_target="tpu_custom_call" | custom-call | tf_op jit(solution)/shard_map/pallas_call | solution.py:180

commit v4 on v3

--- a/solution.py
+++ b/solution.py
@@ -59,54 +59,48 @@
     return jnp.concatenate(rows, axis=0).astype(jnp.bfloat16)
 
 
-def splat_kernel(
-    span,
-    dest_ref,
-    block_ref,
-    count_ref,
-    features_ref,
-    w_in_ref,
-    w_mid_ref,
-    frac_ref,
-    base_ref,
-    sums_ref,
-    hidden_ref,
-    ids_ref,
-    swap_ref,
-):
-    group = sums_ref.shape[2]
-    width = hidden_ref.shape[1] // group
+def splat_slots(count_ref, features_ref, w_in_ref, w_mid_ref, frac_ref, base_ref, hidden_ref, swap_ref):
+    slots = count_ref.shape[0]
+    width = hidden_ref.shape[1] // slots
     half = EDGE * EDGE // PAIR * GZ
-    along, across = TX // EDGE, TY // EDGE
-    start = pl.program_id(0) * group
-    hidden_one = point_layer(w_in_ref[...], features_ref[...])
-    hidden_two = point_layer(w_mid_ref[...], hidden_one)
-    hidden_ref[...] = hidden_two
-    for s in range(group):
-        points = slice(s * width, (s + 1) * width)
-        weights = slot_weights(frac_ref[:, points], base_ref[:, points], count_ref[start + s])
-        sums = lax.dot_general(
-            weights,
-            hidden_two[:, points],
-            (((1,), (1,)), ((), ())),
-            preferred_element_type=jnp.float32,
-        )
-        swap_ref[s * half : (s + 1) * half] = jnp.concatenate([sums[:half], sums[half:]], axis=1)
-        dest, block = dest_ref[start + s], block_ref[start + s]
-        number = lax.rem(block, across) * span + dest * along + lax.div(block, across)
-        ids_ref[s : s + 1] = jnp.full((1, ids_ref.shape[1]), number, jnp.int32)
-    for i in range(EDGE):
-        for jp in range(EDGE // PAIR):
-            for z in range(GZ):
-                row = (i * (EDGE // PAIR) + jp) * GZ + z
-                low = (jp * PAIR + z % PAIR) * LANES
-                sums_ref[z // PAIR, i, :, low : low + LANES] = swap_ref[
-                    pl.ds(row, group, stride=half)
-                ].astype(jnp.bfloat16)
+
+    def one(g, carry):
+        first = g * GROUP
+        points = pl.ds(pl.multiple_of(first * width, GROUP * width), GROUP * width)
+        hidden_one = point_layer(w_in_ref[...], features_ref[:, points])
+        hidden_two = point_layer(w_mid_ref[...], hidden_one)
+        hidden_ref[:, points] = hidden_two
+        offsets, corners = frac_ref[:, points], base_ref[:, points]
+        for s in range(GROUP):
+            part = slice(s * width, (s + 1) * width)
+            weights = slot_weights(offsets[:, part], corners[:, part], count_ref[first + s])
+            sums = lax.dot_general(
+                weights,
+                hidden_two[:, part],
+                (((1,), (1,)), ((), ())),
+                preferred_element_type=jnp.float32,
+            )
+            rows = pl.ds(pl.multiple_of((first + s) * half, half), half)
+            swap_ref[rows] = jnp.concatenate([sums[:half], sums[half:]], axis=1)
+        return carry
+
+    lax.fori_loop(0, slots // GROUP, one, 0)
+
+
+def swap_phase(i, swap_ref, sums_ref):
+    slots = sums_ref.shape[3]
+    half = EDGE * EDGE // PAIR * GZ
+    for jp in range(PAIR):
+        for z in range(GZ):
+            row = (i * PAIR + jp) * GZ + z
+            low = z % PAIR * LANES
+            sums_ref[z // PAIR, i, jp, :, low : low + LANES] = swap_ref[
+                pl.ds(row, slots, stride=half)
+            ].astype(jnp.bfloat16)
 
 
 def interpolate_kernel(count_ref, cells_ref, hidden_ref, frac_ref, base_ref, out_ref, swap_ref):
-    group = cells_ref.shape[2]
+    group = cells_ref.shape[3]
     width = hidden_ref.shape[1] // group
     channels = hidden_ref.shape[0]
     half = EDGE * EDGE // PAIR * GZ
@@ -115,9 +109,9 @@
         for jp in range(EDGE // PAIR):
             for z in range(GZ):
                 row = (i * (EDGE // PAIR) + jp) * GZ + z
-                low = (jp * PAIR + z % PAIR) * LANES
+                low = z % PAIR * LANES
                 swap_ref[row * group : (row + 1) * group] = cells_ref[
-                    z // PAIR, i, :, low : low + LANES
+                    z // PAIR, i, jp, :, low : low + LANES
                 ].astype(jnp.float32)
     for s in range(group):
         points = slice(s * width, (s + 1) * width)
@@ -135,44 +129,6 @@
     return pl.BlockSpec(block, lambda g: tuple(g if d == dimension else 0 for d in range(len(extent))))
 
 
-def whole(extent):
-    return pl.BlockSpec(extent, lambda g: (0,) * len(extent))
-
-
-def splat(features, w_in, w_mid, frac, base, dest, block, count, span):
-    slots, channels = dest.shape[0], w_mid.shape[1]
-    groups = max(1, slots // GROUP)
-    sums = (Z, EDGE, slots, EDGE * PAIR * channels)
-    hidden = (channels, features.shape[1])
-    half = EDGE * EDGE // PAIR * GZ
-    smem = pl.BlockSpec(memory_space=pltpu.SMEM)
-    return pl.pallas_call(
-        functools.partial(splat_kernel, span),
-        grid=(groups,),
-        out_shape=(
-            jax.ShapeDtypeStruct(sums, jnp.bfloat16),
-            jax.ShapeDtypeStruct(hidden, jnp.bfloat16),
-            jax.ShapeDtypeStruct((slots, LANES), jnp.int32),
-        ),
-        in_specs=[
-            smem,
-            smem,
-            smem,
-            grouped(features.shape, 1, groups),
-            whole(w_in.shape),
-            whole(w_mid.shape),
-            grouped(frac.shape, 1, groups),
-            grouped(base.shape, 1, groups),
-        ],
-        out_specs=(
-            grouped(sums, 2, groups),
-            grouped(hidden, 1, groups),
-            grouped((slots, LANES), 0, groups),
-        ),
-        scratch_shapes=[pltpu.VMEM((slots // groups * half, PAIR * channels), jnp.float32)],
-    )(dest, block, count, features, w_in, w_mid, frac, base)
-
-
 def interpolate(cells, hidden, frac, base, count):
     slots, channels = count.shape[0], hidden.shape[0]
     groups = max(1, slots // GROUP)
@@ -183,7 +139,7 @@
         out_shape=jax.ShapeDtypeStruct(hidden.shape, jnp.bfloat16),
         in_specs=[
             pl.BlockSpec(memory_space=pltpu.SMEM),
-            grouped(cells.shape, 2, groups),
+            grouped(cells.shape, 3, groups),
             grouped(hidden.shape, 1, groups),
             grouped(frac.shape, 1, groups),
             grouped(base.shape, 1, groups),
@@ -227,10 +183,22 @@
 
 def conv_kernel(
     sizes,
-    ids_ref,
+    count_ref,
+    dest_ref,
+    block_ref,
+    features_ref,
+    w_in_ref,
+    w_mid_ref,
+    frac_ref,
+    base_ref,
+    w_hbm,
+    out_ref,
+    hidden_out,
+    w_ref,
+    hidden_ref,
+    swap_ref,
     sums_ref,
-    w_ref,
-    out_ref,
+    own_ids,
     ids,
     arrived,
     field,
@@ -257,11 +225,12 @@
     rx_recv,
     rz_send,
     rz_recv,
+    local_sem,
 ):
     rows, columns = sizes
     strips = rows // Z
-    blocks = dense.shape[2]
-    slots = ids.shape[1]
+    blocks = dense.shape[3]
+    slots = sums_ref.shape[3]
     span = (field.shape[4] - blocks) // 2
     layers = field.shape[0]
     me_row, me_column = lax.axis_index("grid"), lax.axis_index("pts")
@@ -285,7 +254,7 @@
 
     def tell(t):
         return pltpu.make_async_remote_copy(
-            src_ref=ids_ref,
+            src_ref=own_ids,
             dst_ref=ids.at[me_row],
             send_sem=id_send.at[t],
             recv_sem=id_recv.at[t],
@@ -293,24 +262,24 @@
             device_id_type=MESH,
         )
 
-    def along_z(i, t):
+    def along_z(i, jp, t):
         z = lax.rem(me_z + t, Z)
         return pltpu.make_async_remote_copy(
-            src_ref=sums_ref.at[z, i],
-            dst_ref=arrived.at[i, me_row],
-            send_sem=z_send.at[i, t],
-            recv_sem=z_recv.at[i, t],
+            src_ref=sums_ref.at[z, i, jp],
+            dst_ref=arrived.at[i, jp, me_row],
+            send_sem=z_send.at[i, jp, t],
+            recv_sem=z_recv.at[i, jp, t],
             device_id=(me_column, z * strips + me_x),
             device_id_type=MESH,
         )
 
-    def along_x(i, t, u):
+    def along_x(i, jp, t, u):
         origin = lax.rem(me_z - t + Z, Z) * strips + me_x
         return pltpu.make_async_remote_copy(
-            src_ref=sums_ref.at[me_z, i] if t == 0 else arrived.at[i, origin],
-            dst_ref=arrived.at[i, origin],
-            send_sem=x_send.at[i, t, u],
-            recv_sem=x_recv.at[i, t, u],
+            src_ref=sums_ref.at[me_z, i, jp] if t == 0 else arrived.at[i, jp, origin],
+            dst_ref=arrived.at[i, jp, origin],
+            send_sem=x_send.at[i, jp, t, u],
+            recv_sem=x_recv.at[i, jp, t, u],
             device_id=(me_column, me_z * strips + lax.rem(me_x + u, strips)),
             device_id_type=MESH,
         )
@@ -337,23 +306,23 @@
             device_id_type=MESH,
         )
 
-    def back_x(i, u):
+    def back_x(i, jp, u):
         return pltpu.make_async_remote_copy(
-            src_ref=dense.at[i, me_strip],
-            dst_ref=dense.at[i, me_strip],
-            send_sem=rx_send.at[i, u],
-            recv_sem=rx_recv.at[i, u],
+            src_ref=dense.at[i, jp, me_strip],
+            dst_ref=dense.at[i, jp, me_strip],
+            send_sem=rx_send.at[i, jp, u],
+            recv_sem=rx_recv.at[i, jp, u],
             device_id=(me_column, me_z * strips + lax.rem(me_x + u, strips)),
             device_id_type=MESH,
         )
 
-    def back_z(i, t):
+    def back_z(i, jp, t):
         z = lax.rem(me_z + t, Z)
         return pltpu.make_async_remote_copy(
-            src_ref=values.at[i, z],
-            dst_ref=out_ref.at[me_z, i],
-            send_sem=rz_send.at[i, t],
-            recv_sem=rz_recv.at[i, t],
+            src_ref=values.at[i, jp, z],
+            dst_ref=out_ref.at[me_z, i, jp],
+            send_sem=rz_send.at[i, jp, t],
+            recv_sem=rz_recv.at[i, jp, t],
             device_id=(me_column, z * strips + me_x),
             device_id_type=MESH,
         )
@@ -401,18 +370,32 @@
         def _():
             pl.semaphore_signal(barrier, inc=1, device_id=(column, row), device_id_type=MESH)
 
+    load = pltpu.make_async_copy(w_hbm, w_ref, local_sem.at[0])
+    load.start()
+    splat_slots(
+        count_ref, features_ref, w_in_ref, w_mid_ref, frac_ref, base_ref, hidden_ref, swap_ref
+    )
+    keep = pltpu.make_async_copy(hidden_ref, hidden_out, local_sem.at[1])
+    keep.start()
+    block = block_ref[...]
+    along, across = TX // EDGE, TY // EDGE
+    number = lax.rem(block, across) * span + dest_ref[...] * along + lax.div(block, across)
+    own_ids[...] = jnp.broadcast_to(number, own_ids.shape)
     pl.semaphore_wait(barrier, expected)
 
     for t in range(1, rows):
         tell(t).start()
     for i in ORDER:
-        for t in (2, 1, 3):
-            along_z(i, t).start()
-        for u in range(1, strips):
-            along_x(i, 0, u).start()
+        swap_phase(i, swap_ref, sums_ref)
+        for jp in range(PAIR):
+            for t in (2, 1, 3):
+                along_z(i, jp, t).start()
+            for u in range(1, strips):
+                along_x(i, jp, 0, u).start()
     for i in ORDER:
-        arrived[i, me_row] = sums_ref[me_z, i]
-    ids[me_row] = ids_ref[...]
+        for jp in range(PAIR):
+            arrived[i, jp, me_row] = sums_ref[me_z, i, jp]
+    ids[me_row] = own_ids[...]
     for k in range(2):
 
         @pl.when(jnp.logical_not(above((-1, 1)[k])))
@@ -428,30 +411,29 @@
     for jp, rows_out in ((0, slice(span + blocks, 2 * span + blocks)), (1, slice(0, span))):
         view = field.at[:, :, jp, :, rows_out]
         view[...] = jnp.zeros(view.shape, field.dtype)
-    build_band(w_ref, band_ref, side_ref)
-    for t in range(1, rows):
-        tell(t).wait_recv()
-
-    def picks(named, first, width):
-        parts = []
-        for low in range(0, width, LANES):
-            place_of = lax.broadcasted_iota(jnp.int32, named.shape, 1) + (low + first)
-            parts.append(jnp.where(named == place_of, 1.0, 0.0))
-        return jnp.concatenate(parts, axis=1)
-
-    for r in range(rows):
-        one_hot = picks(ids[r], me_strip * blocks, blocks)
-        sum_picks[:, r * slots : (r + 1) * slots] = one_hot.T.astype(jnp.bfloat16)
-    for z in range(Z):
-        out_picks[z * slots : (z + 1) * slots] = picks(
-            ids[z * strips + me_x], 0, strips * blocks
-        ).astype(jnp.bfloat16)
+    def picks(r, first, size):
+        named = jnp.broadcast_to(ids[r, 0:1, :slots], (size, slots))
+        place_of = lax.broadcasted_iota(jnp.int32, (size, slots), 0) + first
+        return jnp.where(named == place_of, 1.0, 0.0)
+
+    def build_picks():
+        for t in range(1, rows):
+            tell(t).wait_recv()
+        for r in range(rows):
+            sum_picks[:, r * slots : (r + 1) * slots] = picks(
+                r, me_strip * blocks, blocks
+            ).astype(jnp.bfloat16)
+        for z in range(Z):
+            out_picks[z * slots : (z + 1) * slots] = picks(
+                z * strips + me_x, 0, strips * blocks
+            ).T.astype(jnp.bfloat16)
 
     def forward(i):
-        for t in (1, 2, 3):
-            along_z(i, t).wait_recv()
-            for u in range(1, strips):
-                along_x(i, t, u).start()
+        for jp in range(PAIR):
+            for t in (1, 2, 3):
+                along_z(i, jp, t).wait_recv()
+                for u in range(1, strips):
+                    along_x(i, jp, t, u).start()
 
     def spread(layer, i, tiles):
         for jp in range(PAIR):
@@ -466,20 +448,19 @@
         send_border(layer, i, 0)
 
     def gather(i):
-        for t in range(Z):
-            for u in range(1, strips):
-                along_x(i, t, u).wait_recv()
-        summed = jnp.dot(
-            sum_picks[...],
-            arrived[i].reshape(rows * slots, arrived.shape[3]),
-            preferred_element_type=jnp.float32,
-        ).astype(jnp.bfloat16)
-
-        def tiles(jp, zz):
-            low = (jp * PAIR + zz) * LANES
-            return summed[:, low : low + LANES]
-
-        spread(0, i, tiles)
+        summed = []
+        for jp in range(PAIR):
+            for t in range(Z):
+                for u in range(1, strips):
+                    along_x(i, jp, t, u).wait_recv()
+            summed.append(
+                jnp.dot(
+                    sum_picks[...],
+                    arrived[i, jp].reshape(rows * slots, arrived.shape[4]),
+                    preferred_element_type=jnp.float32,
+                ).astype(jnp.bfloat16)
+            )
+        spread(0, i, lambda jp, zz: summed[jp][:, zz * LANES : (zz + 1) * LANES])
 
     def shifted(tile, down):
         size = tile.shape[0]
@@ -548,17 +529,19 @@
             shift(layer + 1, i, LEVELS[0])
         else:
             for jp in range(PAIR):
-                for zz in range(PAIR):
-                    low = (jp * PAIR + zz) * LANES
-                    dense[i, me_strip, :, low : low + LANES] = tiles(jp, zz)
-            for u in range(1, strips):
-                back_x(i, u).start()
+                dense[i, jp, me_strip] = activated[jp * blocks : (jp + 1) * blocks]
+                for u in range(1, strips):
+                    back_x(i, jp, u).start()
 
     def ready(i, done):
         return {(i - 1) % EDGE, i, (i + 1) % EDGE} <= set(done)
 
     for n, i in enumerate(ORDER):
         forward(i)
+        if n == 0:
+            build_picks()
+            load.wait()
+            build_band(w_ref, band_ref, side_ref)
         if n > 0:
             gather(ORDER[n - 1])
             shift(0, ORDER[n - 1], LEVELS[0])
@@ -608,29 +591,32 @@
         close(OUT_ORDER[-1])
 
     for i in OUT_ORDER:
-        for u in range(1, strips):
-            back_x(i, u).wait_recv()
-        picked = jnp.dot(
-            out_picks[...],
-            dense[i].reshape(strips * blocks, dense.shape[3]),
-            preferred_element_type=jnp.float32,
-        ).astype(jnp.bfloat16)
-        values[i] = picked.reshape(values.shape[1:])
-        for t in (2, 1, 3):
-            back_z(i, t).start()
-        out_ref[me_z, i] = values[i, me_z]
-
+        for jp in range(PAIR):
+            for u in range(1, strips):
+                back_x(i, jp, u).wait_recv()
+            picked = jnp.dot(
+                out_picks[...],
+                dense[i, jp].reshape(strips * blocks, dense.shape[4]),
+                preferred_element_type=jnp.float32,
+            ).astype(jnp.bfloat16)
+            values[i, jp] = picked.reshape(values.shape[2:])
+            for t in (2, 1, 3):
+                back_z(i, jp, t).start()
+            out_ref[me_z, i, jp] = values[i, jp, me_z]
+
+    keep.wait()
     for t in range(1, rows):
         tell(t).wait_send()
     for i in range(EDGE):
-        for t in (1, 2, 3):
-            back_z(i, t).wait_recv()
-            back_z(i, t).wait_send()
-            along_z(i, t).wait_send()
-        for u in range(1, strips):
-            back_x(i, u).wait_send()
-            for t in range(Z):
-                along_x(i, t, u).wait_send()
+        for jp in range(PAIR):
+            for t in (1, 2, 3):
+                back_z(i, jp, t).wait_recv()
+                back_z(i, jp, t).wait_send()
+                along_z(i, jp, t).wait_send()
+            for u in range(1, strips):
+                back_x(i, jp, u).wait_send()
+                for t in range(Z):
+                    along_x(i, jp, t, u).wait_send()
         for layer in range(layers):
             for k in range(2):
 
@@ -644,24 +630,42 @@
                         border(layer, i, part, k).wait_send()
 
 
-def exchange_and_convolve(ids, sums, w_conv):
+def exchange_and_convolve(
+    features, w_in, w_mid, w_conv, frac, base, slot_dest, slot_tile_block, slot_count
+):
     rows, columns = lax.axis_size("grid"), lax.axis_size("pts")
     strips = rows // Z
-    slots, width = sums.shape[2:]
+    slots = slot_count.shape[0]
     layers, channels = w_conv.shape[0], w_conv.shape[4]
+    width = PAIR * PAIR * channels
     span = rows * (TX // EDGE)
     blocks = span * (TY // EDGE) // strips
+    half = EDGE * EDGE // PAIR * GZ
+    hidden = (channels, features.shape[1])
+    cells = (Z, EDGE, PAIR, slots, width)
+    weights = (layers * 27, channels, channels)
     halos = (layers, EDGE, 2)
     borders = halos + (2,)
     dma = pltpu.SemaphoreType.DMA
+    vmem = pl.BlockSpec(memory_space=pltpu.VMEM)
     return pl.pallas_call(
         functools.partial(conv_kernel, (rows, columns)),
-        out_shape=jax.ShapeDtypeStruct(sums.shape, jnp.bfloat16),
-        in_specs=[pl.BlockSpec(memory_space=pltpu.VMEM)] * 3,
-        out_specs=pl.BlockSpec(memory_space=pltpu.VMEM),
+        out_shape=(
+            jax.ShapeDtypeStruct(cells, jnp.bfloat16),
+            jax.ShapeDtypeStruct(hidden, jnp.bfloat16),
+        ),
+        in_specs=[pl.BlockSpec(memory_space=pltpu.SMEM)]
+        + [vmem] * 7
+        + [pl.BlockSpec(memory_space=pl.ANY)],
+        out_specs=(vmem, pl.BlockSpec(memory_space=pl.ANY)),
         scratch_shapes=[
-            pltpu.VMEM((rows, slots, LANES), jnp.int32),
-            pltpu.VMEM((EDGE, rows, slots, width), jnp.bfloat16),
+            pltpu.VMEM(weights, jnp.bfloat16),
+            pltpu.VMEM(hidden, jnp.bfloat16),
+            pltpu.VMEM((slots * half, LANES), jnp.float32),
+            pltpu.VMEM(cells, jnp.bfloat16),
+            pltpu.VMEM((8, slots), jnp.int32),
+            pltpu.VMEM((rows, 8, slots), jnp.int32),
+            pltpu.VMEM((EDGE, PAIR, rows, slots, width), jnp.bfloat16),
             pltpu.VMEM((layers, EDGE + 2, PAIR, PAIR + 2, blocks + 2 * span, LANES), jnp.bfloat16),
             pltpu.VMEM(borders + (span, LANES), jnp.bfloat16),
             pltpu.VMEM((layers, EDGE + 2, 2, 2, span, LANES), jnp.bfloat16),
@@ -670,35 +674,44 @@
             pltpu.VMEM((EDGE, PAIR * blocks, 2 * LANES), jnp.float32),
             pltpu.VMEM((blocks, rows * slots), jnp.bfloat16),
             pltpu.VMEM((Z * slots, strips * blocks), jnp.bfloat16),
-            pltpu.VMEM((EDGE, strips, blocks, width), jnp.bfloat16),
-            pltpu.VMEM((EDGE, Z, slots, width), jnp.bfloat16),
+            pltpu.VMEM((EDGE, PAIR, strips, blocks, width), jnp.bfloat16),
+            pltpu.VMEM((EDGE, PAIR, Z, slots, width), jnp.bfloat16),
             dma((rows,)),
             dma((rows,)),
-            dma((EDGE, Z)),
-            dma((EDGE, Z)),
-            dma((EDGE, Z, strips)),
-            dma((EDGE, Z, strips)),
+            dma((EDGE, PAIR, Z)),
+            dma((EDGE, PAIR, Z)),
+            dma((EDGE, PAIR, Z, strips)),
+            dma((EDGE, PAIR, Z, strips)),
             dma(halos),
             dma(halos),
             dma(borders),
             dma(borders),
-            dma((EDGE, strips)),
-            dma((EDGE, strips)),
-            dma((EDGE, Z)),
-            dma((EDGE, Z)),
+            dma((EDGE, PAIR, strips)),
+            dma((EDGE, PAIR, strips)),
+            dma((EDGE, PAIR, Z)),
+            dma((EDGE, PAIR, Z)),
+            dma((2,)),
         ],
         compiler_params=pltpu.CompilerParams(collective_id=0, has_side_effects=True),
-    )(ids, sums, w_conv.reshape(layers * 27, channels, channels))
+    )(
+        slot_count,
+        slot_dest.reshape(1, slots),
+        slot_tile_block.reshape(1, slots),
+        features,
+        w_in,
+        w_mid,
+        frac,
+        base,
+        w_conv.reshape(weights),
+    )
 
 
 def per_device(
     features, w_in, w_mid, w_conv, point_frac, point_base, slot_dest, slot_tile_block, slot_count
 ):
-    span = lax.axis_size("grid") * (TX // EDGE)
-    sums, hidden, ids = splat(
-        features, w_in, w_mid, point_frac, point_base, slot_dest, slot_tile_block, slot_count, span
+    cells, hidden = exchange_and_convolve(
+        features, w_in, w_mid, w_conv, point_frac, point_base, slot_dest, slot_tile_block, slot_count
     )
-    cells = exchange_and_convolve(ids, sums, w_conv)
     return interpolate(cells, hidden, point_frac, point_base, slot_count)
 
 

time: 114 us -> 101 us (0.89)
  Pallas kernels: 114 us -> 101 us
    pallas_call x1 -> x0, Pallas kernels: 8.64 us -> none  [splat(): pl.pallas_call(functools.partial(splat_kernel, span), grid=(groups,), out...]
    pallas_call x1, Pallas kernels: 99.5 us -> 94.9 us  [exchange_and_convolve(): pl.pallas_call(functools.partial(conv_kernel, (rows, columns)), out_shape...]
where the time goes in v4:
time: 101 us
  Pallas kernels  101 us (100%)
    pallas_call x1, Pallas kernels, exchange_and_convolve(): pl.pallas_call(functools.partial(conv_kernel, (rows, columns)), out_shape...  94.9 us
    pallas_call x1, Pallas kernels, interpolate(): pl.pallas_call(interpolate_kernel, grid=(groups,), out_shape=jax.ShapeDty...  5.85 us

profile of v4, /device:TPU:0, one launch (start us, length us, event | category | flops | bytes accessed | tf_op | source)
XLA Modules:
  0.0 100.8 jit_solution(11267545108772804031)
XLA Ops:
  0.0 94.9 %shard_map.91 = (bf16[4,4,2,64,256]{4,3,2,1,0:T(8,128)(2,1)}, bf16[64,16384]{1,0:T(8,128)(2,1)}) custom-call(s32[64]{0:T(128)} %count_ref.3, s32[1,64]{1,0:T(1,128)} %bitcast.4, s32[1,64]{1,0:T(1,128)} %bitcast.5, bf16[32,16384]{1,0:T(8,128)(2,1)} %features_ref.1, bf16[32,64]{1,0:T(8,128)(2,1)} %w_in_ref.1, bf16[64,64]{1,0:T(8,128)(2,1)} %w_mid_ref.1, ...), custom_call_target="tpu_custom_call" | custom-call | tf_op jit(solution)/shard_map/pallas_call | solution.py:651
  94.9 5.9 %shard_map.92 = bf16[64,16384]{1,0:T(8,128)(2,1)} custom-call(s32[64]{0:T(128)} %count_ref.3, bf16[4,4,2,64,256]{4,3,2,1,0:T(8,128)(2,1)} %get-tuple-element.7.cells_ref, bf16[64,16384]{1,0:T(8,128)(2,1)} %get-tuple-element.8.hidden_ref, f32[3,16384]{1,0:T(4,128)} %frac_ref.3, s32[3,16384]{1,0:T(4,128)} %base_ref.3), custom_call_target="tpu_custom_call" | custom-call | tf_op jit(solution)/shard_map/pallas_call | solution.py:136

commit v5 on v4

--- a/solution.py
+++ b/solution.py
@@ -15,6 +15,7 @@
 PAIR = 2
 Z = GZ // PAIR
 GROUP = 16
+HALVES = 2
 MESH = pl.DeviceIdType.MESH
 LEVELS = ((1, 2), (0, 3))
 ORDER = (3, 0, 1, 2)
@@ -59,7 +60,9 @@
     return jnp.concatenate(rows, axis=0).astype(jnp.bfloat16)
 
 
-def splat_slots(count_ref, features_ref, w_in_ref, w_mid_ref, frac_ref, base_ref, hidden_ref, swap_ref):
+def splat_slots(
+    part, count_ref, features_ref, w_in_ref, w_mid_ref, frac_ref, base_ref, hidden_ref, swap_ref
+):
     slots = count_ref.shape[0]
     width = hidden_ref.shape[1] // slots
     half = EDGE * EDGE // PAIR * GZ
@@ -84,18 +87,19 @@
             swap_ref[rows] = jnp.concatenate([sums[:half], sums[half:]], axis=1)
         return carry
 
-    lax.fori_loop(0, slots // GROUP, one, 0)
-
-
-def swap_phase(i, swap_ref, sums_ref):
+    steps = slots // (GROUP * HALVES)
+    lax.fori_loop(part * steps, (part + 1) * steps, one, 0)
+
+
+def swap_phase(i, part, swap_ref, sums_ref):
     slots = sums_ref.shape[3]
     half = EDGE * EDGE // PAIR * GZ
     for jp in range(PAIR):
         for z in range(GZ):
             row = (i * PAIR + jp) * GZ + z
-            low = z % PAIR * LANES
-            sums_ref[z // PAIR, i, jp, :, low : low + LANES] = swap_ref[
-                pl.ds(row, slots, stride=half)
+            low = (jp * PAIR + z % PAIR) * LANES
+            sums_ref[z // PAIR, i, part, :, low : low + LANES] = swap_ref[
+                pl.ds(part * slots * half + row, slots, stride=half)
             ].astype(jnp.bfloat16)
 
 
@@ -230,7 +234,8 @@
     rows, columns = sizes
     strips = rows // Z
     blocks = dense.shape[3]
-    slots = sums_ref.shape[3]
+    slots = values.shape[3]
+    share = sums_ref.shape[3]
     span = (field.shape[4] - blocks) // 2
     layers = field.shape[0]
     me_row, me_column = lax.axis_index("grid"), lax.axis_index("pts")
@@ -262,24 +267,24 @@
             device_id_type=MESH,
         )
 
-    def along_z(i, jp, t):
+    def along_z(i, h, t):
         z = lax.rem(me_z + t, Z)
         return pltpu.make_async_remote_copy(
-            src_ref=sums_ref.at[z, i, jp],
-            dst_ref=arrived.at[i, jp, me_row],
-            send_sem=z_send.at[i, jp, t],
-            recv_sem=z_recv.at[i, jp, t],
+            src_ref=sums_ref.at[z, i, h],
+            dst_ref=arrived.at[i, h, me_row],
+            send_sem=z_send.at[i, h, t],
+            recv_sem=z_recv.at[i, h, t],
             device_id=(me_column, z * strips + me_x),
             device_id_type=MESH,
         )
 
-    def along_x(i, jp, t, u):
+    def along_x(i, h, t, u):
         origin = lax.rem(me_z - t + Z, Z) * strips + me_x
         return pltpu.make_async_remote_copy(
-            src_ref=sums_ref.at[me_z, i, jp] if t == 0 else arrived.at[i, jp, origin],
-            dst_ref=arrived.at[i, jp, origin],
-            send_sem=x_send.at[i, jp, t, u],
-            recv_sem=x_recv.at[i, jp, t, u],
+            src_ref=sums_ref.at[me_z, i, h] if t == 0 else arrived.at[i, h, origin],
+            dst_ref=arrived.at[i, h, origin],
+            send_sem=x_send.at[i, h, t, u],
+            recv_sem=x_recv.at[i, h, t, u],
             device_id=(me_column, me_z * strips + lax.rem(me_x + u, strips)),
             device_id_type=MESH,
         )
@@ -372,30 +377,28 @@
 
     load = pltpu.make_async_copy(w_hbm, w_ref, local_sem.at[0])
     load.start()
-    splat_slots(
-        count_ref, features_ref, w_in_ref, w_mid_ref, frac_ref, base_ref, hidden_ref, swap_ref
-    )
-    keep = pltpu.make_async_copy(hidden_ref, hidden_out, local_sem.at[1])
-    keep.start()
     block = block_ref[...]
     along, across = TX // EDGE, TY // EDGE
     number = lax.rem(block, across) * span + dest_ref[...] * along + lax.div(block, across)
     own_ids[...] = jnp.broadcast_to(number, own_ids.shape)
-    pl.semaphore_wait(barrier, expected)
-
-    for t in range(1, rows):
-        tell(t).start()
-    for i in ORDER:
-        swap_phase(i, swap_ref, sums_ref)
-        for jp in range(PAIR):
+    ids[me_row] = own_ids[...]
+    keep = pltpu.make_async_copy(hidden_ref, hidden_out, local_sem.at[1])
+    for h in range(HALVES):
+        splat_slots(
+            h, count_ref, features_ref, w_in_ref, w_mid_ref, frac_ref, base_ref, hidden_ref, swap_ref
+        )
+        if h == 0:
+            pl.semaphore_wait(barrier, expected)
+            for t in range(1, rows):
+                tell(t).start()
+        for i in ORDER:
+            swap_phase(i, h, swap_ref, sums_ref)
             for t in (2, 1, 3):
-                along_z(i, jp, t).start()
+                along_z(i, h, t).start()
             for u in range(1, strips):
-                along_x(i, jp, 0, u).start()
-    for i in ORDER:
-        for jp in range(PAIR):
-            arrived[i, jp, me_row] = sums_ref[me_z, i, jp]
-    ids[me_row] = own_ids[...]
+                along_x(i, h, 0, u).start()
+            arrived[i, h, me_row] = sums_ref[me_z, i, h]
+    keep.start()
     for k in range(2):
 
         @pl.when(jnp.logical_not(above((-1, 1)[k])))
@@ -420,20 +423,20 @@
         for t in range(1, rows):
             tell(t).wait_recv()
         for r in range(rows):
-            sum_picks[:, r * slots : (r + 1) * slots] = picks(
-                r, me_strip * blocks, blocks
-            ).astype(jnp.bfloat16)
+            one_hot = picks(r, me_strip * blocks, blocks).astype(jnp.bfloat16)
+            for h in range(HALVES):
+                low = (h * rows + r) * share
+                sum_picks[:, low : low + share] = one_hot[:, h * share : (h + 1) * share]
         for z in range(Z):
             out_picks[z * slots : (z + 1) * slots] = picks(
                 z * strips + me_x, 0, strips * blocks
             ).T.astype(jnp.bfloat16)
 
-    def forward(i):
-        for jp in range(PAIR):
-            for t in (1, 2, 3):
-                along_z(i, jp, t).wait_recv()
-                for u in range(1, strips):
-                    along_x(i, jp, t, u).start()
+    def forward(i, h):
+        for t in (1, 2, 3):
+            along_z(i, h, t).wait_recv()
+            for u in range(1, strips):
+                along_x(i, h, t, u).start()
 
     def spread(layer, i, tiles):
         for jp in range(PAIR):
@@ -448,19 +451,21 @@
         send_border(layer, i, 0)
 
     def gather(i):
-        summed = []
-        for jp in range(PAIR):
+        for h in range(HALVES):
             for t in range(Z):
                 for u in range(1, strips):
-                    along_x(i, jp, t, u).wait_recv()
-            summed.append(
-                jnp.dot(
-                    sum_picks[...],
-                    arrived[i, jp].reshape(rows * slots, arrived.shape[4]),
-                    preferred_element_type=jnp.float32,
-                ).astype(jnp.bfloat16)
-            )
-        spread(0, i, lambda jp, zz: summed[jp][:, zz * LANES : (zz + 1) * LANES])
+                    along_x(i, h, t, u).wait_recv()
+        summed = jnp.dot(
+            sum_picks[...],
+            arrived[i].reshape(rows * slots, arrived.shape[4]),
+            preferred_element_type=jnp.float32,
+        ).astype(jnp.bfloat16)
+
+        def tiles(jp, zz):
+            low = (jp * PAIR + zz) * LANES
+            return summed[:, low : low + LANES]
+
+        spread(0, i, tiles)
 
     def shifted(tile, down):
         size = tile.shape[0]
@@ -485,9 +490,9 @@
                         view = edge_in.at[layer, :, side, part]
                         view[target] = shifted(view[i + 1], down)
 
-    def windows(layer, i, jp, levels):
+    def windows(layer, i, jp, levels, taps):
         parts = []
-        for a in range(3):
+        for a in taps:
             for zl in levels:
                 here = field.at[layer, i + a, :, zl]
                 parts.append(here[jp, inner])
@@ -498,15 +503,18 @@
                 parts.append(jnp.where(low_half, up, down))
         return jnp.concatenate(parts, axis=1)
 
-    def conv_terms(layer, i, part):
-        weight = band_ref[layer, part].reshape(-1, band_ref.shape[5])
+    def conv_terms(layer, i, part, taps):
+        depth = band_ref.shape[5]
+        weight = jnp.concatenate(
+            [band_ref[layer, part, a].reshape(-1, depth) for a in taps], axis=0
+        )
         lhs = jnp.concatenate(
-            [windows(layer, i, jp, LEVELS[part]) for jp in range(PAIR)], axis=0
+            [windows(layer, i, jp, LEVELS[part], taps) for jp in range(PAIR)], axis=0
         )
         return jnp.dot(lhs, weight, preferred_element_type=jnp.float32)
 
     def own_terms(layer, i):
-        totals[i] = conv_terms(layer, i, 0)
+        totals[i] = conv_terms(layer, i, 0, range(3))
 
     def edge_terms(layer, i):
         for side in range(2):
@@ -533,25 +541,27 @@
                 for u in range(1, strips):
                     back_x(i, jp, u).start()
 
-    def ready(i, done):
-        return {(i - 1) % EDGE, i, (i + 1) % EDGE} <= set(done)
-
-    for n, i in enumerate(ORDER):
-        forward(i)
-        if n == 0:
-            build_picks()
-            load.wait()
-            build_band(w_ref, band_ref, side_ref)
-        if n > 0:
-            gather(ORDER[n - 1])
-            shift(0, ORDER[n - 1], LEVELS[0])
+    def near(i):
+        return ((i - 1) % EDGE, i, (i + 1) % EDGE)
+
+    for h in range(HALVES):
+        for n, i in enumerate(ORDER):
+            forward(i, h)
+            if h == 0 and n == 0:
+                build_picks()
+            if h == 0 and n == 1:
+                load.wait()
+                build_band(w_ref, band_ref, side_ref)
+            if h == HALVES - 1 and n > 0:
+                gather(ORDER[n - 1])
+                shift(0, ORDER[n - 1], LEVELS[0])
     for i in OUT_ORDER:
-        if ready(i, ORDER[:-1]):
+        if ORDER[-1] not in near(i):
             own_terms(0, i)
     gather(ORDER[-1])
     shift(0, ORDER[-1], LEVELS[0])
     for i in OUT_ORDER:
-        if not ready(i, ORDER[:-1]):
+        if ORDER[-1] in near(i):
             own_terms(0, i)
 
     for layer in range(layers):
@@ -559,33 +569,38 @@
         if layer > 0:
             for i in OUT_ORDER:
                 own_terms(layer, i)
-        reached, bordered = [], []
-
-        def reach(i):
-            for phase in before:
-                if phase in {(i - 1) % EDGE, i, (i + 1) % EDGE} and phase not in reached:
-                    for k in range(2):
-
-                        @pl.when(above((-1, 1)[k]))
-                        def _():
-                            halo(layer, phase, k).wait_recv()
-
-                    send_border(layer, phase, 1)
-                    shift(layer, phase, LEVELS[1])
-                    reached.append(phase)
+        bordered = []
+
+        def reach(phase):
+            for k in range(2):
+
+                @pl.when(above((-1, 1)[k]))
+                def _():
+                    halo(layer, phase, k).wait_recv()
+
+            send_border(layer, phase, 1)
+            shift(layer, phase, LEVELS[1])
+
+        def add_terms(i, phases):
+            taps = [a for a in range(3) if near(i)[a] in phases]
+            totals[i] += conv_terms(layer, i, 1, taps)
 
         def close(i):
             for phase in before:
-                if phase in {(i - 1) % EDGE, i, (i + 1) % EDGE} and phase not in bordered:
+                if phase in near(i) and phase not in bordered:
                     wait_border(layer, phase)
                     shift_edges(layer, phase)
                     bordered.append(phase)
             edge_terms(layer, i)
             finish(layer, i)
 
+        reached = []
         for n, i in enumerate(OUT_ORDER):
-            reach(i)
-            totals[i] += conv_terms(layer, i, 1)
+            for phase in before:
+                if phase in near(i) and phase not in reached:
+                    reach(phase)
+                    reached.append(phase)
+            add_terms(i, before)
             if n > 0:
                 close(OUT_ORDER[n - 1])
         close(OUT_ORDER[-1])
@@ -612,11 +627,14 @@
             for t in (1, 2, 3):
                 back_z(i, jp, t).wait_recv()
                 back_z(i, jp, t).wait_send()
-                along_z(i, jp, t).wait_send()
             for u in range(1, strips):
                 back_x(i, jp, u).wait_send()
+        for h in range(HALVES):
+            for t in (1, 2, 3):
+                along_z(i, h, t).wait_send()
+            for u in range(1, strips):
                 for t in range(Z):
-                    along_x(i, jp, t, u).wait_send()
+                    along_x(i, h, t, u).wait_send()
         for layer in range(layers):
             for k in range(2):
 
@@ -644,6 +662,7 @@
     hidden = (channels, features.shape[1])
     cells = (Z, EDGE, PAIR, slots, width)
     weights = (layers * 27, channels, channels)
+    share = (HALVES, slots // HALVES, PAIR * width)
     halos = (layers, EDGE, 2)
     borders = halos + (2,)
     dma = pltpu.SemaphoreType.DMA
@@ -662,10 +681,10 @@
             pltpu.VMEM(weights, jnp.bfloat16),
             pltpu.VMEM(hidden, jnp.bfloat16),
             pltpu.VMEM((slots * half, LANES), jnp.float32),
-            pltpu.VMEM(cells, jnp.bfloat16),
+            pltpu.VMEM((Z, EDGE) + share, jnp.bfloat16),
             pltpu.VMEM((8, slots), jnp.int32),
             pltpu.VMEM((rows, 8, slots), jnp.int32),
-            pltpu.VMEM((EDGE, PAIR, rows, slots, width), jnp.bfloat16),
+            pltpu.VMEM((EDGE, HALVES, rows) + share[1:], jnp.bfloat16),
             pltpu.VMEM((layers, EDGE + 2, PAIR, PAIR + 2, blocks + 2 * span, LANES), jnp.bfloat16),
             pltpu.VMEM(borders + (span, LANES), jnp.bfloat16),
             pltpu.VMEM((layers, EDGE + 2, 2, 2, span, LANES), jnp.bfloat16),
@@ -678,10 +697,10 @@
             pltpu.VMEM((EDGE, PAIR, Z, slots, width), jnp.bfloat16),
             dma((rows,)),
             dma((rows,)),
-            dma((EDGE, PAIR, Z)),
-            dma((EDGE, PAIR, Z)),
-            dma((EDGE, PAIR, Z, strips)),
-            dma((EDGE, PAIR, Z, strips)),
+            dma((EDGE, HALVES, Z)),
+            dma((EDGE, HALVES, Z)),
+            dma((EDGE, HALVES, Z, strips)),
+            dma((EDGE, HALVES, Z, strips)),
             dma(halos),
             dma(halos),
             dma(borders),

time: 101 us -> 99.6 us (0.986)
  Pallas kernels: 101 us -> 99.4 us
    pallas_call x1, Pallas kernels: 94.9 us -> 93.5 us  [exchange_and_convolve(): pl.pallas_call(functools.partial(conv_kernel, (rows, columns)), out_shape...]
where the time goes in v5:
time: 99.6 us; the launch traced here: 99.4 us
  Pallas kernels  99.4 us (100%)
    pallas_call x1, Pallas kernels, exchange_and_convolve(): pl.pallas_call(functools.partial(conv_kernel, (rows, columns)), out_shape...  93.5 us
    pallas_call x1, Pallas kernels, interpolate(): pl.pallas_call(interpolate_kernel, grid=(groups,), out_shape=jax.ShapeDty...  5.85 us

profile of v5, /device:TPU:0, one launch (start us, length us, event | category | flops | bytes accessed | tf_op | source)
XLA Modules:
  0.0 99.4 jit_solution(17271729689461378333)
XLA Ops:
  0.0 93.5 %shard_map.91 = (bf16[4,4,2,64,256]{4,3,2,1,0:T(8,128)(2,1)}, bf16[64,16384]{1,0:T(8,128)(2,1)}) custom-call(s32[64]{0:T(128)} %count_ref.3, s32[1,64]{1,0:T(1,128)} %bitcast.4, s32[1,64]{1,0:T(1,128)} %bitcast.5, bf16[32,16384]{1,0:T(8,128)(2,1)} %features_ref.1, bf16[32,64]{1,0:T(8,128)(2,1)} %w_in_ref.1, bf16[64,64]{1,0:T(8,128)(2,1)} %w_mid_ref.1, ...), custom_call_target="tpu_custom_call" | custom-call | tf_op jit(solution)/shard_map/pallas_call | solution.py:670
  93.5 5.9 %shard_map.92 = bf16[64,16384]{1,0:T(8,128)(2,1)} custom-call(s32[64]{0:T(128)} %count_ref.3, bf16[4,4,2,64,256]{4,3,2,1,0:T(8,128)(2,1)} %get-tuple-element.7.cells_ref, bf16[64,16384]{1,0:T(8,128)(2,1)} %get-tuple-element.8.hidden_ref, f32[3,16384]{1,0:T(4,128)} %frac_ref.3, s32[3,16384]{1,0:T(4,128)} %base_ref.3), custom_call_target="tpu_custom_call" | custom-call | tf_op jit(solution)/shard_map/pallas_call | solution.py:140

commit v6 on v5

--- a/solution.py
+++ b/solution.py
@@ -61,7 +61,16 @@
 
 
 def splat_slots(
-    part, count_ref, features_ref, w_in_ref, w_mid_ref, frac_ref, base_ref, hidden_ref, swap_ref
+    part,
+    count_ref,
+    features_ref,
+    w_in_ref,
+    w_mid_ref,
+    frac_ref,
+    base_ref,
+    hidden_ref,
+    weight_ref,
+    swap_ref,
 ):
     slots = count_ref.shape[0]
     width = hidden_ref.shape[1] // slots
@@ -77,6 +86,7 @@
         for s in range(GROUP):
             part = slice(s * width, (s + 1) * width)
             weights = slot_weights(offsets[:, part], corners[:, part], count_ref[first + s])
+            weight_ref[first + s] = weights
             sums = lax.dot_general(
                 weights,
                 hidden_two[:, part],
@@ -103,54 +113,27 @@
             ].astype(jnp.bfloat16)
 
 
-def interpolate_kernel(count_ref, cells_ref, hidden_ref, frac_ref, base_ref, out_ref, swap_ref):
-    group = cells_ref.shape[3]
-    width = hidden_ref.shape[1] // group
+def unswap_piece(i, jp, cells_ref, swap_ref):
+    slots = cells_ref.shape[3]
+    for z in range(GZ):
+        row = (i * PAIR + jp) * GZ + z
+        low = z % PAIR * LANES
+        swap_ref[row * slots : (row + 1) * slots] = cells_ref[
+            z // PAIR, i, jp, :, low : low + LANES
+        ].astype(jnp.float32)
+
+
+def interpolate_slot(s, slots, swap_ref, weight_ref, hidden_ref):
+    width = hidden_ref.shape[1] // slots
     channels = hidden_ref.shape[0]
     half = EDGE * EDGE // PAIR * GZ
-    start = pl.program_id(0) * group
-    for i in range(EDGE):
-        for jp in range(EDGE // PAIR):
-            for z in range(GZ):
-                row = (i * (EDGE // PAIR) + jp) * GZ + z
-                low = z % PAIR * LANES
-                swap_ref[row * group : (row + 1) * group] = cells_ref[
-                    z // PAIR, i, jp, :, low : low + LANES
-                ].astype(jnp.float32)
-    for s in range(group):
-        points = slice(s * width, (s + 1) * width)
-        weights = slot_weights(frac_ref[:, points], base_ref[:, points], count_ref[start + s])
-        cells = swap_ref[pl.ds(s, half, stride=group)].T
-        cells = jnp.concatenate([cells[:channels], cells[channels:]], axis=1).astype(jnp.bfloat16)
-        interp = jnp.dot(cells, weights, preferred_element_type=jnp.float32).astype(jnp.bfloat16)
-        out_ref[:, points] = (
-            hidden_ref[:, points].astype(jnp.float32) + interp.astype(jnp.float32)
-        ).astype(jnp.bfloat16)
-
-
-def grouped(extent, dimension, groups):
-    block = tuple(n // groups if d == dimension else n for d, n in enumerate(extent))
-    return pl.BlockSpec(block, lambda g: tuple(g if d == dimension else 0 for d in range(len(extent))))
-
-
-def interpolate(cells, hidden, frac, base, count):
-    slots, channels = count.shape[0], hidden.shape[0]
-    groups = max(1, slots // GROUP)
-    half = EDGE * EDGE // PAIR * GZ
-    return pl.pallas_call(
-        interpolate_kernel,
-        grid=(groups,),
-        out_shape=jax.ShapeDtypeStruct(hidden.shape, jnp.bfloat16),
-        in_specs=[
-            pl.BlockSpec(memory_space=pltpu.SMEM),
-            grouped(cells.shape, 3, groups),
-            grouped(hidden.shape, 1, groups),
-            grouped(frac.shape, 1, groups),
-            grouped(base.shape, 1, groups),
-        ],
-        out_specs=grouped(hidden.shape, 1, groups),
-        scratch_shapes=[pltpu.VMEM((slots // groups * half, PAIR * channels), jnp.float32)],
-    )(count, cells, hidden, frac, base)
+    points = slice(s * width, (s + 1) * width)
+    cells = swap_ref[pl.ds(s, half, stride=slots)].T
+    cells = jnp.concatenate([cells[:channels], cells[channels:]], axis=1).astype(jnp.bfloat16)
+    interp = jnp.dot(cells, weight_ref[s], preferred_element_type=jnp.float32).astype(jnp.bfloat16)
+    hidden_ref[:, points] = (
+        hidden_ref[:, points].astype(jnp.float32) + interp.astype(jnp.float32)
+    ).astype(jnp.bfloat16)
 
 
 def build_band(w_ref, band_ref, side_ref):
@@ -196,11 +179,12 @@
     frac_ref,
     base_ref,
     w_hbm,
-    out_ref,
-    hidden_out,
+    out_hbm,
     w_ref,
     hidden_ref,
+    weight_ref,
     swap_ref,
+    out_ref,
     sums_ref,
     own_ids,
     ids,
@@ -382,10 +366,18 @@
     number = lax.rem(block, across) * span + dest_ref[...] * along + lax.div(block, across)
     own_ids[...] = jnp.broadcast_to(number, own_ids.shape)
     ids[me_row] = own_ids[...]
-    keep = pltpu.make_async_copy(hidden_ref, hidden_out, local_sem.at[1])
     for h in range(HALVES):
         splat_slots(
-            h, count_ref, features_ref, w_in_ref, w_mid_ref, frac_ref, base_ref, hidden_ref, swap_ref
+            h,
+            count_ref,
+            features_ref,
+            w_in_ref,
+            w_mid_ref,
+            frac_ref,
+            base_ref,
+            hidden_ref,
+            weight_ref,
+            swap_ref,
         )
         if h == 0:
             pl.semaphore_wait(barrier, expected)
@@ -398,7 +390,6 @@
             for u in range(1, strips):
                 along_x(i, h, 0, u).start()
             arrived[i, h, me_row] = sums_ref[me_z, i, h]
-    keep.start()
     for k in range(2):
 
         @pl.when(jnp.logical_not(above((-1, 1)[k])))
@@ -619,13 +610,30 @@
                 back_z(i, jp, t).start()
             out_ref[me_z, i, jp] = values[i, jp, me_z]
 
-    keep.wait()
+    for i in OUT_ORDER:
+        for jp in range(PAIR):
+            for t in (1, 2, 3):
+                back_z(i, jp, t).wait_recv()
+            unswap_piece(i, jp, out_ref, swap_ref)
+
+    def keep(g):
+        width = hidden_ref.shape[1] * GROUP // slots
+        points = slice(g * width, (g + 1) * width)
+        return pltpu.make_async_copy(
+            hidden_ref.at[:, points], out_hbm.at[:, points], local_sem.at[1 + g]
+        )
+
+    for g in range(slots // GROUP):
+        for s in range(g * GROUP, (g + 1) * GROUP):
+            interpolate_slot(s, slots, swap_ref, weight_ref, hidden_ref)
+        keep(g).start()
+    for g in range(slots // GROUP):
+        keep(g).wait()
     for t in range(1, rows):
         tell(t).wait_send()
     for i in range(EDGE):
         for jp in range(PAIR):
             for t in (1, 2, 3):
-                back_z(i, jp, t).wait_recv()
                 back_z(i, jp, t).wait_send()
             for u in range(1, strips):
                 back_x(i, jp, u).wait_send()
@@ -669,18 +677,17 @@
     vmem = pl.BlockSpec(memory_space=pltpu.VMEM)
     return pl.pallas_call(
         functools.partial(conv_kernel, (rows, columns)),
-        out_shape=(
-            jax.ShapeDtypeStruct(cells, jnp.bfloat16),
-            jax.ShapeDtypeStruct(hidden, jnp.bfloat16),
-        ),
+        out_shape=jax.ShapeDtypeStruct(hidden, jnp.bfloat16),
         in_specs=[pl.BlockSpec(memory_space=pltpu.SMEM)]
         + [vmem] * 7
         + [pl.BlockSpec(memory_space=pl.ANY)],
-        out_specs=(vmem, pl.BlockSpec(memory_space=pl.ANY)),
+        out_specs=pl.BlockSpec(memory_space=pl.ANY),
         scratch_shapes=[
             pltpu.VMEM(weights, jnp.bfloat16),
             pltpu.VMEM(hidden, jnp.bfloat16),
+            pltpu.VMEM((slots, PAIR * half, hidden[1] // slots), jnp.bfloat16),
             pltpu.VMEM((slots * half, LANES), jnp.float32),
+            pltpu.VMEM(cells, jnp.bfloat16),
             pltpu.VMEM((Z, EDGE) + share, jnp.bfloat16),
             pltpu.VMEM((8, slots), jnp.int32),
             pltpu.VMEM((rows, 8, slots), jnp.int32),
@@ -709,34 +716,32 @@
             dma((EDGE, PAIR, strips)),
             dma((EDGE, PAIR, Z)),
             dma((EDGE, PAIR, Z)),
-            dma((2,)),
+            dma((1 + slots // GROUP,)),
         ],
-        compiler_params=pltpu.CompilerParams(collective_id=0, has_side_effects=True),
+        compiler_params=pltpu.CompilerParams(
+            collective_id=0, has_side_effects=True, vmem_limit_bytes=52 << 20
+        ),
     )(
-        slot_count,
-        slot_dest.reshape(1, slots),
-        slot_tile_block.reshape(1, slots),
-        features,
-        w_in,
-        w_mid,
-        frac,
-        base,
-        w_conv.reshape(weights),
+        *(
+            pltpu.with_memory_space_constraint(operand, pltpu.HBM)
+            for operand in (
+                slot_count,
+                slot_dest.reshape(1, slots),
+                slot_tile_block.reshape(1, slots),
+                features,
+                w_in,
+                w_mid,
+                frac,
+                base,
+                w_conv.reshape(weights),
+            )
+        )
     )
-
-
-def per_device(
-    features, w_in, w_mid, w_conv, point_frac, point_base, slot_dest, slot_tile_block, slot_count
-):
-    cells, hidden = exchange_and_convolve(
-        features, w_in, w_mid, w_conv, point_frac, point_base, slot_dest, slot_tile_block, slot_count
-    )
-    return interpolate(cells, hidden, point_frac, point_base, slot_count)
 
 
 def solution(mesh):
     return jax.shard_map(
-        per_device,
+        exchange_and_convolve,
         mesh=mesh,
         in_specs=(
             P(None, ("pts", "grid")),

time: 99.6 us -> 99.2 us (level)
  Pallas kernels: 99.4 us -> 96 us
  local copies, waits for them, and re-layouts: 0 us -> 3.05 us
    pallas_call x1 -> x0, Pallas kernels: 5.85 us -> none  [interpolate(): pl.pallas_call(interpolate_kernel, grid=(groups,), out_shape=jax.ShapeDty...]
    unnamed x0 -> x1, local copies, waits for them, and re-layouts: none -> 3.05 us
    pallas_call x1, Pallas kernels: 93.5 us -> 96 us  [exchange_and_convolve(): pl.pallas_call(functools.partial(conv_kernel, (rows, columns)), out_shape...]
where the time goes in v6:
time: 99.2 us; the launch traced here: 99 us
  Pallas kernels  96 us (97%)
  local copies, waits for them, and re-layouts  3.05 us (3%)
    pallas_call x1, Pallas kernels, exchange_and_convolve(): pl.pallas_call(functools.partial(conv_kernel, (rows, columns)), out_shape...  96 us
    unnamed x1, local copies, waits for them, and re-layouts  3.05 us

profile of v6, /device:TPU:0, one launch (start us, length us, event | category | flops | bytes accessed | tf_op | source)
XLA Modules:
  0.0 99.0 jit_solution(2449692920330735830)
XLA Ops:
  0.0 96.0 %shard_map.91 = bf16[64,16384]{1,0:T(8,128)(2,1)} custom-call(s32[64]{0:T(128)} %count_ref.1, s32[1,64]{1,0:T(1,128)} %bitcast.4, s32[1,64]{1,0:T(1,128)} %bitcast.5, bf16[32,16384]{1,0:T(8,128)(2,1)} %features_ref.1, bf16[32,64]{1,0:T(8,128)(2,1)} %w_in_ref.1, bf16[64,64]{1,0:T(8,128)(2,1)} %w_mid_ref.1, f32[3,16384]{1,0:T(4,128)} %frac_ref.1, ...), custom_call_target="tpu_custom_call" | custom-call | tf_op jit(solution)/shard_map/pallas_call | solution.py:678
  96.0 3.0 %copy.11 = bf16[64,16384]{1,0:T(8,128)(2,1)} copy(bf16[64,16384]{1,0:T(8,128)(2,1)} %shard_map.91) | data formatting | bytes 4194304

commit v7 on v6

--- a/solution.py
+++ b/solution.py
@@ -719,7 +719,7 @@
             dma((1 + slots // GROUP,)),
         ],
         compiler_params=pltpu.CompilerParams(
-            collective_id=0, has_side_effects=True, vmem_limit_bytes=52 << 20
+            collective_id=0, has_side_effects=True, vmem_limit_bytes=46 << 20
         ),
     )(
         *(

time: 99.2 us -> 97.4 us (0.982)
  local copies, waits for them, and re-layouts: 3.05 us -> 1.32 us
    unnamed x1, local copies, waits for them, and re-layouts: 3.05 us -> 1.32 us
where the time goes in v7:
time: 97.4 us; the launch traced here: 97.3 us
  Pallas kernels  95.9 us (98%)
  local copies, waits for them, and re-layouts  1.32 us (1%)
    pallas_call x1, Pallas kernels, exchange_and_convolve(): pl.pallas_call(functools.partial(conv_kernel, (rows, columns)), out_shape...  95.9 us

profile of v7, /device:TPU:0, one launch (start us, length us, event | category | flops | bytes accessed | tf_op | source)
XLA Modules:
  0.0 97.3 jit_solution(2287521687607980321)
XLA Ops:
  0.0 95.9 %shard_map.91 = bf16[64,16384]{1,0:T(8,128)(2,1)S(1)} custom-call(s32[64]{0:T(128)} %count_ref.1, s32[1,64]{1,0:T(1,128)} %bitcast.4, s32[1,64]{1,0:T(1,128)} %bitcast.5, bf16[32,16384]{1,0:T(8,128)(2,1)} %features_ref.1, bf16[32,64]{1,0:T(8,128)(2,1)} %w_in_ref.1, bf16[64,64]{1,0:T(8,128)(2,1)} %w_mid_ref.1, f32[3,16384]{1,0:T(4,128)} %frac_ref.1, ...), custom_call_target="tpu_custom_call" | custom-call | tf_op jit(solution)/shard_map/pallas_call | solution.py:678
  96.0 1.3 %copy.11 = bf16[64,16384]{1,0:T(8,128)(2,1)} copy(bf16[64,16384]{1,0:T(8,128)(2,1)S(1)} %shard_map.91) | data formatting | bytes 4194304

commit v8 on v7

--- a/solution.py
+++ b/solution.py
@@ -380,11 +380,14 @@
             swap_ref,
         )
         if h == 0:
+            for i in ORDER:
+                swap_phase(i, h, swap_ref, sums_ref)
             pl.semaphore_wait(barrier, expected)
             for t in range(1, rows):
                 tell(t).start()
         for i in ORDER:
-            swap_phase(i, h, swap_ref, sums_ref)
+            if h > 0:
+                swap_phase(i, h, swap_ref, sums_ref)
             for t in (2, 1, 3):
                 along_z(i, h, t).start()
             for u in range(1, strips):
@@ -424,7 +427,7 @@
             ).T.astype(jnp.bfloat16)
 
     def forward(i, h):
-        for t in (1, 2, 3):
+        for t in (2, 1, 3):
             along_z(i, h, t).wait_recv()
             for u in range(1, strips):
                 along_x(i, h, t, u).start()

time: 97.4 us -> 98.2 us (level)
  no operation moved by 1% of the time
where the time goes in v8:
time: 98.2 us; the launch traced here: 98.1 us
  Pallas kernels  96.7 us (98%)
  local copies, waits for them, and re-layouts  1.32 us (1%)
    pallas_call x1, Pallas kernels, exchange_and_convolve(): pl.pallas_call(functools.partial(conv_kernel, (rows, columns)), out_shape...  96.7 us

profile of v8, /device:TPU:0, one launch (start us, length us, event | category | flops | bytes accessed | tf_op | source)
XLA Modules:
  0.0 98.1 jit_solution(1607052998936358881)
XLA Ops:
  0.0 96.7 %shard_map.91 = bf16[64,16384]{1,0:T(8,128)(2,1)S(1)} custom-call(s32[64]{0:T(128)} %count_ref.1, s32[1,64]{1,0:T(1,128)} %bitcast.4, s32[1,64]{1,0:T(1,128)} %bitcast.5, bf16[32,16384]{1,0:T(8,128)(2,1)} %features_ref.1, bf16[32,64]{1,0:T(8,128)(2,1)} %w_in_ref.1, bf16[64,64]{1,0:T(8,128)(2,1)} %w_mid_ref.1, f32[3,16384]{1,0:T(4,128)} %frac_ref.1, ...), custom_call_target="tpu_custom_call" | custom-call | tf_op jit(solution)/shard_map/pallas_call | solution.py:681
  96.7 1.3 %copy.11 = bf16[64,16384]{1,0:T(8,128)(2,1)} copy(bf16[64,16384]{1,0:T(8,128)(2,1)S(1)} %shard_map.91) | data formatting | bytes 4194304
